TPU v7x, 32 devices: a whole 2x2x4 slice. The times are simulated.
32 devices in a mesh: gy: 4 (over z), gz: 8 (over y, x, core).
Axes of the slice: x: 2, y: 2, z: 4, core: 2. Of those that a mesh axis runs over, the one named last changes fastest.
Arguments:
- data_weight: float32 [320, 160, 640], P('gy', 'gz'), may hold values from 0.25 to 4
- blob_taps: float32 [3, 7], replicated, may hold values from 0.2 to 1
Outputs:
- new_weight: float32 [320, 160, 640], P('gy', 'gz')
- changes: float32 [3], replicated
All inputs are finite; a program needn't handle non-finite values.
Results may differ from a plain program's by a relative error of at most 0.00002.
Values sent between devices are 32-bit elements; how exact they have to be, the bound alone decides.
No kernel may reach another device: no remote copies, remote signals or barrier semaphores. Data moves between devices by JAX's collectives and lax.ppermute only.
A program may use at most 64 MiB of HBM per device.

v0:
```python
import jax
import jax.numpy as jnp
from jax import lax
from jax.sharding import PartitionSpec as P

RAD = 3
ITERS = 3


def with_halo(cells, sides, width):
    for axis, dim in sides:
        count = lax.axis_size(axis)
        ends = count - 1
        head = lax.slice_in_dim(cells, 0, width, axis=dim)
        tail = lax.slice_in_dim(cells, cells.shape[dim] - width, cells.shape[dim], axis=dim)
        cells = jnp.concatenate(
            [
                lax.ppermute(tail, axis, [(i, (i + 1) % count) for i in range(ends)]),
                cells,
                lax.ppermute(head, axis, [((i + 1) % count, i) for i in range(ends)]),
            ],
            axis=dim,
        )
    return cells


def smear_valid(padded, kernel, axis_dim):
    length = padded.shape[axis_dim] - 2 * RAD
    result = kernel[0] * lax.slice_in_dim(padded, 0, length, axis=axis_dim)
    for offset in range(1, 2 * RAD + 1):
        result = result + kernel[offset] * lax.slice_in_dim(
            padded, offset, offset + length, axis=axis_dim
        )
    return result


def smear_local(field, kernel):
    padded = jnp.pad(field, ((0, 0), (0, 0), (RAD, RAD)))
    return smear_valid(padded, kernel, 2)


def shards(data_weight, blob_taps):
    kernel = blob_taps / jnp.sum(blob_taps, axis=1, keepdims=True)
    changes = []
    weight = jnp.ones_like(data_weight)
    for iteration in range(ITERS):
        product = weight * data_weight
        blurred = smear_local(product, kernel[2])
        padded = with_halo(blurred, (("gy", 0),), RAD)
        blurred = smear_valid(padded, kernel[0], 0)
        padded = with_halo(blurred, (("gz", 1),), RAD)
        blurred = smear_valid(padded, kernel[1], 1)
        weight = weight / blurred
        deviation = jnp.max(jnp.abs(blurred - 1.0))
        changes.append(lax.pmax(deviation, ("gy", "gz")))
    result_max = jnp.stack(changes)
    return (weight, result_max)


def solution(mesh):
    return jax.shard_map(
        shards,
        mesh=mesh,
        in_specs=(P("gy", "gz", None), P()),
        out_specs=(P("gy", "gz", None), P()),
        check_vma=False,
    )
```

profile of v0, /device:TPU:0, one launch (start us, length us, event | category | flops | bytes accessed | tf_op | source)
XLA Modules:
  0.0 279.0 jit_solution(5993323312113206324)
XLA Ops:
  0.6 0.8 reduce_sum.9
  1.4 0.8 broadcast_divide_fusion
  2.2 0.5 fusion.142
  2.7 0.7 fusion.141
  3.4 21.3 %fusion.90 = f32[80,20,640]{2,0,1:T(8,128)S(1)} fusion(f32[80,20,640]{2,0,1:T(8,128)} %param.2, f32[]{:T(128)} %bitcast.8, f32[]{:T(128)} %bitcast.7, f32[]{:T(128)} %bitcast.6, f32[]{:T(128)} %bitcast.5, f32[]{:T(128)} %bitcast.4, f32[]{:T(128)} %bitcast.3, f32[]{:T(128)} %bitcast.2), kind=kLoop, calls=%fused_computation.156 | loop fusion | flops 13312000 | bytes 8192028 | tf_op jit(solution)/shard_map/add | solution.py:31
  24.7 0.1 fusion.140
  24.8 5.0 %collective-permute-start = (f32[3,20,640]{2,0,1:T(4,128)S(1)}, f32[3,20,640]{2,0,1:T(4,128)S(1)}, u32[]{:S(2)}, u32[]{:S(2)}) collective-permute-start(f32[3,20,640]{2,0,1:T(4,128)S(1)} %get-tuple-element.23), channel_id=1, source_target_pairs={{0,8},{8,16},{16,24},{1,9},{9,17},{17,25},{2,10},{10,18},{18,26},{... | collective-permute-start | bytes 460808 | tf_op jit(solution)/shard_map/ppermute | solution.py:18
  29.8 1.3 collective-permute-start.1
  31.1 3.0 %collective-permute-done = f32[3,20,640]{2,0,1:T(4,128)S(1)} collective-permute-done((f32[3,20,640]{2,0,1:T(4,128)S(1)}, f32[3,20,640]{2,0,1:T(4,128)S(1)}, u32[]{:S(2)}, u32[]{:S(2)}) %collective-permute-start) | collective-permute-done | bytes 153632 | tf_op jit(solution)/shard_map/ppermute | solution.py:18
  34.1 4.1 %collective-permute-done.1 = f32[3,20,640]{2,0,1:T(4,128)S(1)} collective-permute-done((f32[3,20,640]{2,0,1:T(4,128)S(1)}, f32[3,20,640]{2,0,1:T(4,128)S(1)}, u32[]{:S(2)}, u32[]{:S(2)}) %collective-permute-start.1) | collective-permute-done | bytes 153632 | tf_op jit(solution)/shard_map/ppermute | solution.py:20
  38.2 8.2 %fusion.31 = f32[80,20,640]{2,0,1:T(8,128)S(1)} fusion(f32[80,20,640]{2,0,1:T(8,128)S(1)} %fusion.90, f32[3,20,640]{2,0,1:T(4,128)S(1)} %collective-permute-done.1, f32[3,20,640]{2,0,1:T(4,128)S(1)} %collective-permute-done, f32[]{:T(128)} %bitcast.14, f32[]{:T(128)} %bitcast.13, f32[]{:T(128)} %bitcast.12, f32[]{:T(128)} %bitcast.11, f32[]{:T(128)} %bitcast.10, ...), kind=kLoop, calls=%fused_computation.97 | loop fusion | flops 19456000 | bytes 8499228 | tf_op jit(solution)/shard_map/add | solution.py:31
  46.4 0.0 copy-start.1
  46.4 0.1 fusion.139
  46.5 1.3 collective-permute-start.2
  47.8 1.3 collective-permute-start.3
  49.1 0.3 collective-permute-done.2
  49.5 4.0 %collective-permute-done.3 = f32[80,3,640]{2,0,1:T(8,128)S(1)} collective-permute-done((f32[80,3,640]{2,0,1:T(8,128)S(1)}, f32[80,3,640]{2,0,1:T(8,128)S(1)}, u32[]{:S(2)}, u32[]{:S(2)}) %collective-permute-start.3) | collective-permute-done | bytes 614432 | tf_op jit(solution)/shard_map/ppermute | solution.py:20
  53.5 0.0 copy-done.1
  53.5 0.0 copy-start
  53.5 16.5 %abs_reduce_fusion.2 = (f32[]{:T(128)}, f32[80,20,640]{2,0,1:T(8,128)S(1)}) fusion(f32[80,3,640]{2,0,1:T(8,128)S(1)} %collective-permute-done.3, f32[80,20,640]{2,0,1:T(8,128)} %copy-done.1, f32[]{:T(128)} %bitcast.20, f32[]{:T(128)} %bitcast.19, f32[]{:T(128)} %bitcast.18, f32[]{:T(128)} %bitcast.17, f32[80,3,640]{2,0,1:T(8,128)S(1)} %collective-permute-done.2, ...), kind=kLoop, calls=%fused_computation.212 | loop fusion | flops 22528000 | bytes 9420832 | tf_op jit(solution)/shard_map/reduce_max | solution.py:54
  70.0 0.0 copy-done
  70.0 2.5 divide_multiply_fusion.1
  72.5 21.1 %fusion.102 = f32[80,20,640]{2,0,1:T(8,128)S(1)} fusion(f32[80,20,640]{2,0,1:T(8,128)} %divide_multiply_fusion.1, f32[]{:T(128)} %bitcast.8, f32[]{:T(128)} %bitcast.7, f32[]{:T(128)} %bitcast.6, f32[]{:T(128)} %bitcast.5, f32[]{:T(128)} %bitcast.4, f32[]{:T(128)} %bitcast.3, f32[]{:T(128)} %bitcast.2), kind=kLoop, calls=%fused_computation.168 | loop fusion | flops 13312000 | bytes 8192028 | tf_op jit(solution)/shard_map/add | solution.py:31
  93.6 0.1 fusion.138
  93.7 3.5 %collective-permute-start.4 = (f32[3,20,640]{2,0,1:T(4,128)S(1)}, f32[3,20,640]{2,0,1:T(4,128)S(1)}, u32[]{:S(2)}, u32[]{:S(2)}) collective-permute-start(f32[3,20,640]{2,0,1:T(4,128)S(1)} %get-tuple-element.19), channel_id=1, source_target_pairs={{0,8},{8,16},{16,24},{1,9},{9,17},{17,25},{2,10},{10,18},{18,26},{... | collective-permute-start | bytes 460808 | tf_op jit(solution)/shard_map/ppermute | solution.py:18
  97.2 1.3 collective-permute-start.5
  98.5 1.9 collective-permute-done.4
  100.4 4.4 %collective-permute-done.5 = f32[3,20,640]{2,0,1:T(4,128)S(1)} collective-permute-done((f32[3,20,640]{2,0,1:T(4,128)S(1)}, f32[3,20,640]{2,0,1:T(4,128)S(1)}, u32[]{:S(2)}, u32[]{:S(2)}) %collective-permute-start.5) | collective-permute-done | bytes 153632 | tf_op jit(solution)/shard_map/ppermute | solution.py:20
  104.8 8.2 %fusion.17 = f32[80,20,640]{2,0,1:T(8,128)S(1)} fusion(f32[80,20,640]{2,0,1:T(8,128)S(1)} %fusion.102, f32[3,20,640]{2,0,1:T(4,128)S(1)} %collective-permute-done.5, f32[3,20,640]{2,0,1:T(4,128)S(1)} %collective-permute-done.4, f32[]{:T(128)} %bitcast.14, f32[]{:T(128)} %bitcast.13, f32[]{:T(128)} %bitcast.12, f32[]{:T(128)} %bitcast.11, f32[]{:T(128)} %bitcast.10, ...), kind=kLoop, calls=%fused_computation.83 | loop fusion | flops 19456000 | bytes 8499228 | tf_op jit(solution)/shard_map/add | solution.py:31
  113.1 0.0 copy-start.2
  113.1 2.0 copy-done.2
  115.0 0.1 fusion.137
  115.1 12.6 %collective-permute-start.6 = (f32[80,3,640]{2,0,1:T(8,128)S(1)}, f32[80,3,640]{2,0,1:T(8,128)S(1)}, u32[]{:S(2)}, u32[]{:S(2)}) collective-permute-start(f32[80,3,640]{2,0,1:T(8,128)S(1)} %get-tuple-element.17), channel_id=1, source_target_pairs={{0,1},{1,2},{2,3},{3,4},{4,5},{5,6},{6,7},{8,9},{9,10},{10,11},{11... | collective-permute-start | bytes 1843208 | tf_op jit(solution)/shard_map/ppermute | solution.py:18
  127.7 1.3 collective-permute-start.7
  129.0 0.3 collective-permute-done.6
  129.3 4.7 %collective-permute-done.7 = f32[80,3,640]{2,0,1:T(8,128)S(1)} collective-permute-done((f32[80,3,640]{2,0,1:T(8,128)S(1)}, f32[80,3,640]{2,0,1:T(8,128)S(1)}, u32[]{:S(2)}, u32[]{:S(2)}) %collective-permute-start.7) | collective-permute-done | bytes 614432 | tf_op jit(solution)/shard_map/ppermute | solution.py:20
  134.0 17.7 %abs_reduce_fusion.1 = (f32[]{:T(128)}, f32[80,20,640]{2,0,1:T(8,128)}) fusion(f32[80,3,640]{2,0,1:T(8,128)S(1)} %collective-permute-done.7, f32[80,20,640]{2,0,1:T(8,128)} %copy-done.2, f32[]{:T(128)} %bitcast.20, f32[]{:T(128)} %bitcast.19, f32[]{:T(128)} %bitcast.18, f32[]{:T(128)} %bitcast.17, f32[80,3,640]{2,0,1:T(8,128)S(1)} %collective-permute-done.6, ...), kind=kLoop, calls=%fused_computation.211 | loop fusion | flops 22528000 | bytes 9420832 | tf_op jit(solution)/shard_map/reduce_max | solution.py:54
  151.7 6.3 %divide_multiply_fusion = (f32[80,20,640]{2,0,1:T(8,128)}, f32[80,20,640]{2,0,1:T(8,128)}) fusion(f32[80,20,640]{2,0,1:T(8,128)S(1)} %copy-done, f32[80,20,640]{2,0,1:T(8,128)S(1)} %get-tuple-element.6, f32[80,20,640]{2,0,1:T(8,128)} %get-tuple-element.8), kind=kLoop, calls=%fused_computation.214 | loop fusion | flops 3072000 | bytes 20480000 | tf_op jit(solution)/shard_map/mul | solution.py:47
  158.0 21.1 %fusion.114 = f32[80,20,640]{2,0,1:T(8,128)S(1)} fusion(f32[80,20,640]{2,0,1:T(8,128)} %get-tuple-element.11, f32[]{:T(128)} %bitcast.8, f32[]{:T(128)} %bitcast.7, f32[]{:T(128)} %bitcast.6, f32[]{:T(128)} %bitcast.5, f32[]{:T(128)} %bitcast.4, f32[]{:T(128)} %bitcast.3, f32[]{:T(128)} %bitcast.2), kind=kLoop, calls=%fused_computation.180 | loop fusion | flops 13312000 | bytes 8192028 | tf_op jit(solution)/shard_map/add | solution.py:31
  179.1 0.1 fusion.136
  179.1 3.5 %collective-permute-start.8 = (f32[3,20,640]{2,0,1:T(4,128)S(1)}, f32[3,20,640]{2,0,1:T(4,128)S(1)}, u32[]{:S(2)}, u32[]{:S(2)}) collective-permute-start(f32[3,20,640]{2,0,1:T(4,128)S(1)} %get-tuple-element.15), channel_id=1, source_target_pairs={{0,8},{8,16},{16,24},{1,9},{9,17},{17,25},{2,10},{10,18},{18,26},{... | collective-permute-start | bytes 460808 | tf_op jit(solution)/shard_map/ppermute | solution.py:18
  182.6 1.3 collective-permute-start.9
  183.9 1.9 collective-permute-done.8
  185.9 4.4 %collective-permute-done.9 = f32[3,20,640]{2,0,1:T(4,128)S(1)} collective-permute-done((f32[3,20,640]{2,0,1:T(4,128)S(1)}, f32[3,20,640]{2,0,1:T(4,128)S(1)}, u32[]{:S(2)}, u32[]{:S(2)}) %collective-permute-start.9) | collective-permute-done | bytes 153632 | tf_op jit(solution)/shard_map/ppermute | solution.py:20
  190.3 8.2 %fusion.3 = f32[80,20,640]{2,0,1:T(8,128)S(1)} fusion(f32[80,20,640]{2,0,1:T(8,128)S(1)} %fusion.114, f32[3,20,640]{2,0,1:T(4,128)S(1)} %collective-permute-done.9, f32[3,20,640]{2,0,1:T(4,128)S(1)} %collective-permute-done.8, f32[]{:T(128)} %bitcast.14, f32[]{:T(128)} %bitcast.13, f32[]{:T(128)} %bitcast.12, f32[]{:T(128)} %bitcast.11, f32[]{:T(128)} %bitcast.10, ...), kind=kLoop, calls=%fused_computation.69 | loop fusion | flops 19456000 | bytes 8499228 | tf_op jit(solution)/shard_map/add | solution.py:31
  198.5 0.1 fusion.135
  198.6 11.1 %collective-permute-start.10 = (f32[80,3,640]{2,0,1:T(8,128)S(1)}, f32[80,3,640]{2,0,1:T(8,128)S(1)}, u32[]{:S(2)}, u32[]{:S(2)}) collective-permute-start(f32[80,3,640]{2,0,1:T(8,128)S(1)} %get-tuple-element.13), channel_id=1, source_target_pairs={{0,1},{1,2},{2,3},{3,4},{4,5},{5,6},{6,7},{8,9},{9,10},{10,11},{11... | collective-permute-start | bytes 1843208 | tf_op jit(solution)/shard_map/ppermute | solution.py:18
  209.7 0.0 copy-start.3
  209.8 1.6 collective-permute-start.11
  211.3 0.0 collective-permute-done.10
  211.4 3.3 %collective-permute-done.11 = f32[80,3,640]{2,0,1:T(8,128)S(1)} collective-permute-done((f32[80,3,640]{2,0,1:T(8,128)S(1)}, f32[80,3,640]{2,0,1:T(8,128)S(1)}, u32[]{:S(2)}, u32[]{:S(2)}) %collective-permute-start.11) | collective-permute-done | bytes 614432 | tf_op jit(solution)/shard_map/ppermute | solution.py:20
  214.7 11.4 %abs_reduce_fusion = (f32[]{:T(128)}, f32[80,20,640]{2,0,1:T(8,128)}) fusion(f32[80,3,640]{2,0,1:T(8,128)S(1)} %collective-permute-done.11, f32[80,20,640]{2,0,1:T(8,128)S(1)} %fusion.3, f32[]{:T(128)} %bitcast.20, f32[]{:T(128)} %bitcast.19, f32[]{:T(128)} %bitcast.18, f32[]{:T(128)} %bitcast.17, f32[80,3,640]{2,0,1:T(8,128)S(1)} %collective-permute-done.10, ...), kind=kLoop, calls=%fused_computation.210 | loop fusion | flops 22528000 | bytes 9420832 | tf_op jit(solution)/shard_map/reduce_max | solution.py:54
  226.1 0.0 copy-done.3
  226.1 4.7 %multiply_divide_fusion = f32[80,20,640]{2,0,1:T(8,128)} fusion(f32[80,20,640]{2,0,1:T(8,128)S(1)} %copy-done.3, f32[80,20,640]{2,0,1:T(8,128)} %get-tuple-element.10), kind=kLoop, calls=%fused_computation.213 | loop fusion | flops 2048000 | bytes 12288000 | tf_op jit(solution)/shard_map/div | solution.py:53
  230.8 45.7 %all-reduce.3 = (f32[1]{0:T(128)}, f32[1]{0:T(128)}, f32[1]{0:T(128)}) all-reduce(f32[1]{0:T(128)} %bitcast.23, f32[1]{0:T(128)} %bitcast.22, f32[1]{0:T(128)} %bitcast.21), channel_id=1, replica_groups=mesh['gy'=4,'gz'=8] {'gy','gz'}, use_global_device_ids=true, to_apply=%region_6.7 | all-reduce | flops 3 | bytes 24 | tf_op jit(solution)/shard_map/pmax | solution.py:55
  276.5 2.5 pad_maximum_fusion.12
Async XLA Ops:
  24.8 9.3 %collective-permute-start = (f32[3,20,640]{2,0,1:T(4,128)S(1)}, f32[3,20,640]{2,0,1:T(4,128)S(1)}, u32[]{:S(2)}, u32[]{:S(2)}) collective-permute-start(f32[3,20,640]{2,0,1:T(4,128)S(1)} %get-tuple-element.23), channel_id=1, source_target_pairs={{0,8},{8,16},{16,24},{1,9},{9,17},{17,25},{2,10},{10,18},{18,26},{... | collective-permute-start | bytes 460808 | tf_op jit(solution)/shard_map/ppermute | solution.py:18
  29.8 8.4 %collective-permute-start.1 = (f32[3,20,640]{2,0,1:T(4,128)S(1)}, f32[3,20,640]{2,0,1:T(4,128)S(1)}, u32[]{:S(2)}, u32[]{:S(2)}) collective-permute-start(f32[3,20,640]{2,0,1:T(4,128)S(1)} %get-tuple-element.24), channel_id=1, source_target_pairs={{8,0},{16,8},{24,16},{9,1},{17,9},{25,17},{10,2},{18,10},{26,18},{... | collective-permute-start | bytes 460808 | tf_op jit(solution)/shard_map/ppermute | solution.py:20
  46.4 7.1 %copy-start.1 = (f32[80,20,640]{2,0,1:T(8,128)}, f32[80,20,640]{2,0,1:T(8,128)S(1)}, u32[]{:S(2)}) copy-start(f32[80,20,640]{2,0,1:T(8,128)S(1)} %fusion.31) | copy-start | bytes 12288004
  46.5 2.9 %collective-permute-start.2 = (f32[80,3,640]{2,0,1:T(8,128)S(1)}, f32[80,3,640]{2,0,1:T(8,128)S(1)}, u32[]{:S(2)}, u32[]{:S(2)}) collective-permute-start(f32[80,3,640]{2,0,1:T(8,128)S(1)} %get-tuple-element.21), channel_id=1, source_target_pairs={{0,1},{1,2},{2,3},{3,4},{4,5},{5,6},{6,7},{8,9},{9,10},{10,11},{11... | collective-permute-start | bytes 1843208 | tf_op jit(solution)/shard_map/ppermute | solution.py:18
  47.8 5.6 %collective-permute-start.3 = (f32[80,3,640]{2,0,1:T(8,128)S(1)}, f32[80,3,640]{2,0,1:T(8,128)S(1)}, u32[]{:S(2)}, u32[]{:S(2)}) collective-permute-start(f32[80,3,640]{2,0,1:T(8,128)S(1)} %get-tuple-element.22), channel_id=1, source_target_pairs={{1,0},{2,1},{3,2},{4,3},{5,4},{6,5},{7,6},{9,8},{10,9},{11,10},{12... | collective-permute-start | bytes 1843208 | tf_op jit(solution)/shard_map/ppermute | solution.py:20
  53.5 16.5 %copy-start = (f32[80,20,640]{2,0,1:T(8,128)S(1)}, f32[80,20,640]{2,0,1:T(8,128)}, u32[]{:S(2)}) copy-start(f32[80,20,640]{2,0,1:T(8,128)} %param.2) | copy-start | bytes 12288004
  93.7 6.7 %collective-permute-start.4 = (f32[3,20,640]{2,0,1:T(4,128)S(1)}, f32[3,20,640]{2,0,1:T(4,128)S(1)}, u32[]{:S(2)}, u32[]{:S(2)}) collective-permute-start(f32[3,20,640]{2,0,1:T(4,128)S(1)} %get-tuple-element.19), channel_id=1, source_target_pairs={{0,8},{8,16},{16,24},{1,9},{9,17},{17,25},{2,10},{10,18},{18,26},{... | collective-permute-start | bytes 460808 | tf_op jit(solution)/shard_map/ppermute | solution.py:18
  97.2 7.7 %collective-permute-start.5 = (f32[3,20,640]{2,0,1:T(4,128)S(1)}, f32[3,20,640]{2,0,1:T(4,128)S(1)}, u32[]{:S(2)}, u32[]{:S(2)}) collective-permute-start(f32[3,20,640]{2,0,1:T(4,128)S(1)} %get-tuple-element.20), channel_id=1, source_target_pairs={{8,0},{16,8},{24,16},{9,1},{17,9},{25,17},{10,2},{18,10},{26,18},{... | collective-permute-start | bytes 460808 | tf_op jit(solution)/shard_map/ppermute | solution.py:20
  113.1 2.0 copy-start.2
  115.1 14.2 %collective-permute-start.6 = (f32[80,3,640]{2,0,1:T(8,128)S(1)}, f32[80,3,640]{2,0,1:T(8,128)S(1)}, u32[]{:S(2)}, u32[]{:S(2)}) collective-permute-start(f32[80,3,640]{2,0,1:T(8,128)S(1)} %get-tuple-element.17), channel_id=1, source_target_pairs={{0,1},{1,2},{2,3},{3,4},{4,5},{5,6},{6,7},{8,9},{9,10},{10,11},{11... | collective-permute-start | bytes 1843208 | tf_op jit(solution)/shard_map/ppermute | solution.py:18
  127.7 6.3 %collective-permute-start.7 = (f32[80,3,640]{2,0,1:T(8,128)S(1)}, f32[80,3,640]{2,0,1:T(8,128)S(1)}, u32[]{:S(2)}, u32[]{:S(2)}) collective-permute-start(f32[80,3,640]{2,0,1:T(8,128)S(1)} %get-tuple-element.18), channel_id=1, source_target_pairs={{1,0},{2,1},{3,2},{4,3},{5,4},{6,5},{7,6},{9,8},{10,9},{11,10},{12... | collective-permute-start | bytes 1843208 | tf_op jit(solution)/shard_map/ppermute | solution.py:20
  179.1 6.7 %collective-permute-start.8 = (f32[3,20,640]{2,0,1:T(4,128)S(1)}, f32[3,20,640]{2,0,1:T(4,128)S(1)}, u32[]{:S(2)}, u32[]{:S(2)}) collective-permute-start(f32[3,20,640]{2,0,1:T(4,128)S(1)} %get-tuple-element.15), channel_id=1, source_target_pairs={{0,8},{8,16},{16,24},{1,9},{9,17},{17,25},{2,10},{10,18},{18,26},{... | collective-permute-start | bytes 460808 | tf_op jit(solution)/shard_map/ppermute | solution.py:18
  182.6 7.7 %collective-permute-start.9 = (f32[3,20,640]{2,0,1:T(4,128)S(1)}, f32[3,20,640]{2,0,1:T(4,128)S(1)}, u32[]{:S(2)}, u32[]{:S(2)}) collective-permute-start(f32[3,20,640]{2,0,1:T(4,128)S(1)} %get-tuple-element.16), channel_id=1, source_target_pairs={{8,0},{16,8},{24,16},{9,1},{17,9},{25,17},{10,2},{18,10},{26,18},{... | collective-permute-start | bytes 460808 | tf_op jit(solution)/shard_map/ppermute | solution.py:20
  198.6 12.7 %collective-permute-start.10 = (f32[80,3,640]{2,0,1:T(8,128)S(1)}, f32[80,3,640]{2,0,1:T(8,128)S(1)}, u32[]{:S(2)}, u32[]{:S(2)}) collective-permute-start(f32[80,3,640]{2,0,1:T(8,128)S(1)} %get-tuple-element.13), channel_id=1, source_target_pairs={{0,1},{1,2},{2,3},{3,4},{4,5},{5,6},{6,7},{8,9},{9,10},{10,11},{11... | collective-permute-start | bytes 1843208 | tf_op jit(solution)/shard_map/ppermute | solution.py:18
  209.7 16.4 %copy-start.3 = (f32[80,20,640]{2,0,1:T(8,128)S(1)}, f32[80,20,640]{2,0,1:T(8,128)}, u32[]{:S(2)}) copy-start(f32[80,20,640]{2,0,1:T(8,128)} %get-tuple-element.12) | copy-start | bytes 12288004
  209.8 4.9 %collective-permute-start.11 = (f32[80,3,640]{2,0,1:T(8,128)S(1)}, f32[80,3,640]{2,0,1:T(8,128)S(1)}, u32[]{:S(2)}, u32[]{:S(2)}) collective-permute-start(f32[80,3,640]{2,0,1:T(8,128)S(1)} %get-tuple-element.14), channel_id=1, source_target_pairs={{1,0},{2,1},{3,2},{4,3},{5,4},{6,5},{7,6},{9,8},{10,9},{11,10},{12... | collective-permute-start | bytes 1843208 | tf_op jit(solution)/shard_map/ppermute | solution.py:20
where the time goes:
time: 280 us; the launch traced here: 279 us
  other arithmetic  151 us (54%)
  blocking collectives  45.7 us (16%)
  starting transfers between devices  45 us (16%)
  waiting for transfers between devices  32.6 us (12%)
  local copies, waits for them, and re-layouts  3.7 us (1%)
    add x6, other arithmetic, smear_valid(): result + kernel[offset] * lax.slice_in_dim(padded, offset, offset + lengt...  88 us
    pmax x1, blocking collectives, shards(): changes.append(lax.pmax(deviation, ('gy', 'gz')))  45.7 us
    reduce_max x3, other arithmetic, shards(): deviation = jnp.max(jnp.abs(blurred - 1.0))  45.7 us
    ppermute x6, starting transfers between devices, with_halo(): lax.ppermute(tail, axis, [(i, (i + 1) % count) for i in range(ends)])  37 us
    ppermute x6, waiting for transfers between devices, with_halo(): lax.ppermute(head, axis, [((i + 1) % count, i) for i in range(ends)])  25 us
    mul x2, other arithmetic, shards(): product = weight * data_weight  8.77 us
    ppermute x6, starting transfers between devices, with_halo(): lax.ppermute(head, axis, [((i + 1) % count, i) for i in range(ends)])  8.02 us
    ppermute x6, waiting for transfers between devices, with_halo(): lax.ppermute(tail, axis, [(i, (i + 1) % count) for i in range(ends)])  7.55 us
  transfers between devices with their start and end apart: 12, of which 11 were waited for; matrix products, arithmetic and copies ran while one was open for 0% of the time, Pallas kernels for 0%

commit v1 on v0

v1 whole, which is shorter than its diff:
```python
import functools

import jax
import jax.numpy as jnp
from jax import lax
from jax.experimental import pallas as pl
from jax.experimental.pallas import tpu as pltpu
from jax.sharding import PartitionSpec as P

RAD = 3
ITERS = 3
LANES = 128
ROWS = 8


def smear_x(row, taps):
    length = row.shape[1]
    padded = jnp.concatenate([row, jnp.zeros((row.shape[0], LANES), row.dtype)], axis=1)
    total = length + LANES
    result = taps[RAD] * row
    for k in range(2 * RAD + 1):
        if k != RAD:
            moved = pltpu.roll(padded, (RAD - k) % total, 1)
            result = result + taps[k] * moved[:, :length]
    return result


def smear_x_all(src, dst, taps):
    planes, height, _ = src.shape
    chunk = 2 * ROWS if height % (2 * ROWS) == 0 else ROWS

    def body(z, _):
        for y in range(0, height, chunk):
            dst[z, y : y + chunk, :] = smear_x(src[z, y : y + chunk, :], taps)
        return 0

    lax.fori_loop(0, planes, body, 0)


def first_kernel(kernel_ref, d_ref, u_ref):
    taps = [kernel_ref[2, k] for k in range(2 * RAD + 1)]
    smear_x_all(d_ref, u_ref, taps)


def step_kernel(last, *refs):
    if last:
        kernel_ref, p_ref, u_ref, zlo_ref, zhi_ref, tail_ref, d_ref, out_ref, dev_ref, ext = refs
    else:
        kernel_ref, p_ref, u_ref, zlo_ref, zhi_ref, tail_ref, out_ref, unext_ref, dev_ref, ext = refs
    planes, height, length = p_ref.shape
    ntaps = 2 * RAD + 1
    ky = [kernel_ref[0, k] for k in range(ntaps)]
    kz = [kernel_ref[1, k] for k in range(ntaps)]
    total = height + ROWS

    def fill(z, _):
        ext[z + RAD, 0:height, :] = u_ref[z]
        return 0

    lax.fori_loop(0, planes, fill, 0)

    def fill_tail(z, _):
        ext[z, height:total, :] = tail_ref[z]
        return 0

    lax.fori_loop(0, planes + 2 * RAD, fill_tail, 0)
    for z in range(RAD):
        ext[z, 0:height, :] = zlo_ref[z]
        ext[planes + RAD + z, 0:height, :] = zhi_ref[z]

    dev_ref[...] = jnp.zeros_like(dev_ref)
    for x in range(0, length, LANES):
        cols = slice(x, x + LANES)

        def body(z, _, cols=cols):
            v = kz[0] * ext[z, :, cols]
            for k in range(1, ntaps):
                v = v + kz[k] * ext[z + k, :, cols]
            b = ky[RAD] * v[:height]
            for k in range(ntaps):
                if k != RAD:
                    b = b + ky[k] * pltpu.roll(v, (RAD - k) % total, 0)[:height]
            p = p_ref[z, :, cols]
            if last:
                out_ref[z, :, cols] = p / (b * d_ref[z, :, cols])
            else:
                out_ref[z, :, cols] = p / b
            off = jnp.max(jnp.abs(b - 1.0).reshape(height // ROWS, ROWS, LANES), axis=0)
            dev_ref[...] = jnp.maximum(dev_ref[...], off)
            return 0

        lax.fori_loop(0, planes, body, 0)
    if not last:
        smear_x_all(out_ref, unext_ref, [kernel_ref[2, k] for k in range(ntaps)])


def exchange(u):
    ny = lax.axis_size("gy")
    nz = lax.axis_size("gz")
    planes, height, _ = u.shape

    def move(block, dy, dz):
        pairs = []
        for y in range(ny):
            for z in range(nz):
                if 0 <= y + dy < ny and 0 <= z + dz < nz:
                    pairs.append(((y + dy) * nz + z + dz, y * nz + z))
        return lax.ppermute(block, ("gy", "gz"), pairs)

    lo = slice(0, RAD)
    zend = slice(planes - RAD, planes)
    yend = slice(height - RAD, height)
    zlo = move(u[zend], 0, -1)
    zhi = move(u[lo], 0, 1)
    ylo = jnp.concatenate(
        [move(u[zend, yend], -1, -1), move(u[:, yend], -1, 0), move(u[lo, yend], -1, 1)], axis=0
    )
    yhi = jnp.concatenate(
        [move(u[zend, lo], 1, -1), move(u[:, lo], 1, 0), move(u[lo, lo], 1, 1)], axis=0
    )
    gap = jnp.zeros((ylo.shape[0], ROWS - 2 * RAD, ylo.shape[2]), u.dtype)
    tail = jnp.concatenate([yhi, gap, ylo], axis=1)
    return zlo, zhi, tail


def shards(data_weight, blob_taps):
    kernel = blob_taps / jnp.sum(blob_taps, axis=1, keepdims=True)
    d = jnp.transpose(data_weight, (1, 0, 2))
    planes, height, length = d.shape
    vmem = pl.BlockSpec(memory_space=pltpu.VMEM)
    smem = pl.BlockSpec(memory_space=pltpu.SMEM)
    whole = jax.ShapeDtypeStruct(d.shape, d.dtype)
    dev_shape = jax.ShapeDtypeStruct((ROWS, LANES), d.dtype)
    ext = pltpu.VMEM((planes + 2 * RAD, height + ROWS, length), d.dtype)
    params = pltpu.CompilerParams(vmem_limit_bytes=56 * 1024 * 1024)
    u = pl.pallas_call(
        first_kernel, out_shape=whole, in_specs=[smem, vmem], out_specs=vmem, compiler_params=params, name="first"
    )(kernel, d)
    p = d
    devs = []
    for iteration in range(ITERS):
        last = iteration == ITERS - 1
        zlo, zhi, tail = exchange(u)
        args = [kernel, p, u, zlo, zhi, tail] + ([d] if last else [])
        outs = pl.pallas_call(
            functools.partial(step_kernel, last),
            out_shape=[whole, dev_shape] if last else [whole, whole, dev_shape],
            in_specs=[smem] + [vmem] * (len(args) - 1),
            out_specs=[vmem] * (2 if last else 3),
            scratch_shapes=[ext],
            compiler_params=params,
            name="step",
        )(*args)
        if last:
            weight, dev = outs
        else:
            p, u, dev = outs
        devs.append(dev)
    local = jnp.max(jnp.stack(devs), axis=(1, 2))
    return jnp.transpose(weight, (1, 0, 2)), lax.pmax(local, ("gy", "gz"))


def solution(mesh):
    return jax.shard_map(
        shards,
        mesh=mesh,
        in_specs=(P("gy", "gz", None), P()),
        out_specs=(P("gy", "gz", None), P()),
        check_vma=False,
    )
```

time: 280 us -> 241 us (0.86)
  other arithmetic: 151 us -> 5.76 us
  Pallas kernels: 0 us -> 70.1 us
  starting transfers between devices: 45 us -> 85.8 us
  waiting for transfers between devices: 32.6 us -> 19.1 us
  local copies, waits for them, and re-layouts: 3.7 us -> 14.3 us
    add x6 -> x0, other arithmetic: 88 us -> none  [smear_valid(): result + kernel[offset] * lax.slice_in_dim(padded, offset, offset + lengt...]
    pallas_call x0 -> x4, Pallas kernels: none -> 70.1 us  [the longest x3 58 us: shards(): pl.pallas_call(functools.partial(step_kernel, last), out_shape=[whole, de...]
    reduce_max x3 -> x1, other arithmetic: 45.7 us -> 0.79 us  [shards(): local = jnp.max(jnp.stack(devs), axis=(1, 2))]
    ppermute x12 -> x24, starting transfers between devices: 45 us -> 85.8 us  [move(): return lax.ppermute(block, ('gy', 'gz'), pairs)]
    ppermute x12 -> x24, waiting for transfers between devices: 32.6 us -> 19.1 us  [move(): return lax.ppermute(block, ('gy', 'gz'), pairs)]
    mul x2 -> x0, other arithmetic: 8.77 us -> none  [shards(): product = weight * data_weight]
    slice x8 -> x9, local copies, waits for them, and re-layouts: 1.71 us -> 10.5 us  [the longest x3 4.01 us: exchange(): zhi = move(u[lo], 0, 1)]
    div x1 -> x0, other arithmetic: 4.68 us -> none  [shards(): weight = weight / blurred]
  transfers between devices with their start and end apart: 12 -> 24, of which waited for: 11 -> 6; matrix products, arithmetic and copies ran while one was open for 0% -> 4% of each run, Pallas kernels for 0% -> 0%
where the time goes in v1:
time: 241 us; the launch traced here: 240 us
  starting transfers between devices  85.8 us (36%)
  Pallas kernels  70.1 us (29%)
  blocking collectives  44 us (18%)
  waiting for transfers between devices  19.1 us (8%)
  local copies, waits for them, and re-layouts  14.3 us (6%)
  other arithmetic  5.76 us (2%)
    ppermute x24, starting transfers between devices, move(): return lax.ppermute(block, ('gy', 'gz'), pairs)  85.8 us
    pallas_call x3, Pallas kernels, shards(): pl.pallas_call(functools.partial(step_kernel, last), out_shape=[whole, de...  58 us
    pmax x1, blocking collectives, shards(): return (jnp.transpose(weight, (1, 0, 2)), lax.pmax(local, ('gy', 'gz')))  44 us
    ppermute x24, waiting for transfers between devices, move(): return lax.ppermute(block, ('gy', 'gz'), pairs)  19.1 us
    pallas_call x1, Pallas kernels, shards(): pl.pallas_call(first_kernel, out_shape=whole, in_specs=[smem, vmem], out_...  12 us
  transfers between devices with their start and end apart: 24, of which 6 were waited for; matrix products, arithmetic and copies ran while one was open for 4% of the time, Pallas kernels for 0%

profile of v1, /device:TPU:0, one launch (start us, length us, event | category | flops | bytes accessed | tf_op | source)
XLA Modules:
  0.0 240.0 jit_solution(7718049379684220110)
XLA Ops:
  0.6 0.8 reduce_sum.9
  1.4 1.3 broadcast_divide_fusion.kernel_ref.refs_0_
  2.8 12.0 %first.1.refs_2_ = f32[20,80,640]{2,1,0:T(8,128)} custom-call(f32[3,7]{1,0:T(4,128)} %broadcast_divide_fusion.kernel_ref.refs_0_, f32[20,80,640]{2,1,0:T(8,128)} %bitcast.5), custom_call_target="tpu_custom_call" | custom-call | tf_op jit(solution)/shard_map/first/pallas_call | solution.py:136
  14.8 1.3 fusion.8
  16.1 1.3 collective-permute-start.1
  17.4 3.1 %collective-permute-start = (f32[3,80,640]{2,1,0:T(8,128)S(1)}, f32[3,80,640]{2,1,0:T(8,128)S(1)}, u32[]{:S(2)}, u32[]{:S(2)}) collective-permute-start(f32[3,80,640]{2,1,0:T(8,128)S(1)} %get-tuple-element.41), channel_id=1, source_target_pairs={{0,1},{1,2},{2,3},{3,4},{4,5},{5,6},{6,7},{8,9},{9,10},{10,11},{11... | collective-permute-start | bytes 1843208 | tf_op jit(solution)/shard_map/ppermute | solution.py:108
  20.5 1.2 fusion.7
  21.7 1.3 collective-permute-start.3
  23.0 5.6 %collective-permute-start.6 = (f32[20,3,640]{2,1,0:T(4,128)S(1)}, f32[20,3,640]{2,1,0:T(4,128)S(1)}, u32[]{:S(2)}, u32[]{:S(2)}) collective-permute-start(f32[20,3,640]{2,1,0:T(4,128)S(1)} %get-tuple-element.39), channel_id=1, source_target_pairs={{0,8},{1,9},{2,10},{3,11},{4,12},{5,13},{6,14},{7,15},{8,16},{9,17... | collective-permute-start | bytes 460808 | tf_op jit(solution)/shard_map/ppermute | solution.py:108
  28.6 0.9 fusion.6
  29.6 0.7 collective-permute-start.2
  30.2 0.0 collective-permute-done.2
  30.3 0.7 collective-permute-start.7
  30.9 0.0 collective-permute-done.7
  30.9 14.2 %collective-permute-start.5 = (f32[3,3,640]{2,1,0:T(4,128)S(1)}, f32[3,3,640]{2,1,0:T(4,128)S(1)}, u32[]{:S(2)}, u32[]{:S(2)}) collective-permute-start(f32[3,3,640]{2,1,0:T(4,128)S(1)} %get-tuple-element.36), channel_id=1, source_target_pairs={{0,9},{1,10},{2,11},{3,12},{4,13},{5,14},{6,15},{8,17},{9,18},{10,... | collective-permute-start | bytes 69128 | tf_op jit(solution)/shard_map/ppermute | solution.py:108
  45.2 1.6 collective-permute-done.5
  46.7 1.3 collective-permute-start.4
  48.0 0.1 pad.20.clone
  48.1 4.0 %collective-permute-done.4 = f32[3,3,640]{2,1,0:T(4,128)S(1)} collective-permute-done((f32[3,3,640]{2,1,0:T(4,128)S(1)}, f32[3,3,640]{2,1,0:T(4,128)S(1)}, u32[]{:S(2)}, u32[]{:S(2)}) %collective-permute-start.4) | collective-permute-done | bytes 23072 | tf_op jit(solution)/shard_map/ppermute | solution.py:108
  52.1 0.0 collective-permute-done.3
  52.1 0.0 collective-permute-done.6
  52.1 1.0 maximum_maximum_fusion.refs_5_
  53.0 0.9 copy-done
  53.9 0.8 copy-done.2
  54.7 21.8 %step.3 = (f32[20,80,640]{2,1,0:T(8,128)}, f32[20,80,640]{2,1,0:T(8,128)}, f32[8,128]{1,0:T(8,128)}) custom-call(f32[3,7]{1,0:T(4,128)} %broadcast_divide_fusion.kernel_ref.refs_0_, f32[20,80,640]{2,1,0:T(8,128)} %bitcast.6, f32[20,80,640]{2,1,0:T(8,128)} %first.1.refs_2_, f32[3,80,640]{2,1,0:T(8,128)} %copy-done.2, f32[3,80,640]{2,1,0:T(8,128)} %copy-done, ...), custom_call_target="tpu_custom_call" | custom-call | tf_op jit(solution)/shard_map/step/pallas_call | solution.py:145
  76.5 1.3 fusion.5
  77.9 1.3 collective-permute-start.9
  79.2 5.1 %collective-permute-start.8 = (f32[3,80,640]{2,1,0:T(8,128)S(1)}, f32[3,80,640]{2,1,0:T(8,128)S(1)}, u32[]{:S(2)}, u32[]{:S(2)}) collective-permute-start(f32[3,80,640]{2,1,0:T(8,128)S(1)} %get-tuple-element.33), channel_id=1, source_target_pairs={{0,1},{1,2},{2,3},{3,4},{4,5},{5,6},{6,7},{8,9},{9,10},{10,11},{11... | collective-permute-start | bytes 1843208 | tf_op jit(solution)/shard_map/ppermute | solution.py:108
  84.3 1.2 fusion.4
  85.5 1.3 collective-permute-start.11
  86.8 4.6 %collective-permute-start.14 = (f32[20,3,640]{2,1,0:T(4,128)S(1)}, f32[20,3,640]{2,1,0:T(4,128)S(1)}, u32[]{:S(2)}, u32[]{:S(2)}) collective-permute-start(f32[20,3,640]{2,1,0:T(4,128)S(1)} %get-tuple-element.31), channel_id=1, source_target_pairs={{0,8},{1,9},{2,10},{3,11},{4,12},{5,13},{6,14},{7,15},{8,16},{9,17... | collective-permute-start | bytes 460808 | tf_op jit(solution)/shard_map/ppermute | solution.py:108
  91.4 0.9 fusion.3
  92.3 0.7 collective-permute-start.10
  93.0 0.7 collective-permute-start.15
  93.7 13.4 %collective-permute-start.13 = (f32[3,3,640]{2,1,0:T(4,128)S(1)}, f32[3,3,640]{2,1,0:T(4,128)S(1)}, u32[]{:S(2)}, u32[]{:S(2)}) collective-permute-start(f32[3,3,640]{2,1,0:T(4,128)S(1)} %get-tuple-element.28), channel_id=1, source_target_pairs={{0,9},{1,10},{2,11},{3,12},{4,13},{5,14},{6,15},{8,17},{9,18},{10,... | collective-permute-start | bytes 69128 | tf_op jit(solution)/shard_map/ppermute | solution.py:108
  107.1 1.6 collective-permute-done.13
  108.6 1.3 collective-permute-start.12
  109.9 5.2 %collective-permute-done.12 = f32[3,3,640]{2,1,0:T(4,128)S(1)} collective-permute-done((f32[3,3,640]{2,1,0:T(4,128)S(1)}, f32[3,3,640]{2,1,0:T(4,128)S(1)}, u32[]{:S(2)}, u32[]{:S(2)}) %collective-permute-start.12) | collective-permute-done | bytes 23072 | tf_op jit(solution)/shard_map/ppermute | solution.py:108
  115.1 0.0 collective-permute-done.11
  115.1 0.0 collective-permute-done.14
  115.1 0.9 maximum_maximum_fusion.1.refs_5_
  116.0 0.0 copy-start.5
  116.1 0.8 copy-done.3
  116.9 0.2 copy-done.5
  117.1 21.8 %step.4 = (f32[20,80,640]{2,1,0:T(8,128)}, f32[20,80,640]{2,1,0:T(8,128)}, f32[8,128]{1,0:T(8,128)}) custom-call(f32[3,7]{1,0:T(4,128)} %broadcast_divide_fusion.kernel_ref.refs_0_, f32[20,80,640]{2,1,0:T(8,128)} %get-tuple-element.10.refs_1_, f32[20,80,640]{2,1,0:T(8,128)} %get-tuple-element.11.refs_2_, f32[3,80,640]{2,1,0:T(8,128)} %copy-done.5, ...), custom_call_target="tpu_custom_call" | custom-call | tf_op jit(solution)/shard_map/step/pallas_call | solution.py:145
  138.9 1.3 fusion.2
  140.2 1.3 collective-permute-start.17
  141.5 6.4 %collective-permute-start.16 = (f32[3,80,640]{2,1,0:T(8,128)S(1)}, f32[3,80,640]{2,1,0:T(8,128)S(1)}, u32[]{:S(2)}, u32[]{:S(2)}) collective-permute-start(f32[3,80,640]{2,1,0:T(8,128)S(1)} %get-tuple-element.25), channel_id=1, source_target_pairs={{0,1},{1,2},{2,3},{3,4},{4,5},{5,6},{6,7},{8,9},{9,10},{10,11},{11... | collective-permute-start | bytes 1843208 | tf_op jit(solution)/shard_map/ppermute | solution.py:108
  147.9 1.2 fusion.1
  149.1 1.3 collective-permute-start.19
  150.4 4.6 %collective-permute-start.22 = (f32[20,3,640]{2,1,0:T(4,128)S(1)}, f32[20,3,640]{2,1,0:T(4,128)S(1)}, u32[]{:S(2)}, u32[]{:S(2)}) collective-permute-start(f32[20,3,640]{2,1,0:T(4,128)S(1)} %get-tuple-element.23), channel_id=1, source_target_pairs={{0,8},{1,9},{2,10},{3,11},{4,12},{5,13},{6,14},{7,15},{8,16},{9,17... | collective-permute-start | bytes 460808 | tf_op jit(solution)/shard_map/ppermute | solution.py:108
  155.0 0.9 fusion
  155.9 0.7 collective-permute-start.18
  156.6 0.7 collective-permute-start.23
  157.3 13.3 %collective-permute-start.21 = (f32[3,3,640]{2,1,0:T(4,128)S(1)}, f32[3,3,640]{2,1,0:T(4,128)S(1)}, u32[]{:S(2)}, u32[]{:S(2)}) collective-permute-start(f32[3,3,640]{2,1,0:T(4,128)S(1)} %get-tuple-element.20), channel_id=1, source_target_pairs={{0,9},{1,10},{2,11},{3,12},{4,13},{5,14},{6,15},{8,17},{9,18},{10,... | collective-permute-start | bytes 69128 | tf_op jit(solution)/shard_map/ppermute | solution.py:108
  170.6 1.6 collective-permute-done.21
  172.2 1.3 collective-permute-start.20
  173.5 5.3 %collective-permute-done.20 = f32[3,3,640]{2,1,0:T(4,128)S(1)} collective-permute-done((f32[3,3,640]{2,1,0:T(4,128)S(1)}, f32[3,3,640]{2,1,0:T(4,128)S(1)}, u32[]{:S(2)}, u32[]{:S(2)}) %collective-permute-start.20) | collective-permute-done | bytes 23072 | tf_op jit(solution)/shard_map/ppermute | solution.py:108
  178.7 0.9 maximum_maximum_fusion.2.refs_5_
  179.7 0.8 copy-done.1
  180.5 0.3 copy-done.4
  180.8 14.5 %step.5 = (f32[20,80,640]{2,1,0:T(8,128)}, f32[8,128]{1,0:T(8,128)}) custom-call(f32[3,7]{1,0:T(4,128)} %broadcast_divide_fusion.kernel_ref.refs_0_, f32[20,80,640]{2,1,0:T(8,128)} %get-tuple-element.12.refs_1_, f32[20,80,640]{2,1,0:T(8,128)} %get-tuple-element.13.refs_2_, f32[3,80,640]{2,1,0:T(8,128)} %copy-done.4, f32[3,80,640]{2,1,0:T(8,128)} %copy-done.1, ...), custom_call_target="tpu_custom_call" | custom-call | tf_op jit(solution)/shard_map/step/pallas_call | solution.py:145
  195.2 0.8 maximum_reduce_fusion
  196.0 44.0 %pmax.7 = f32[3]{0:T(128)} all-reduce(f32[3]{0:T(128)S(1)} %maximum_reduce_fusion), channel_id=1, replica_groups=mesh['gy'=4,'gz'=8] {'gy','gz'}, use_global_device_ids=true, to_apply=%region_2.0 | all-reduce | flops 3 | bytes 24 | tf_op jit(solution)/shard_map/pmax | solution.py:160
  (22 shorter events, 0.0 us)
Async XLA Ops:
  16.1 36.9 %collective-permute-start.1 = (f32[3,80,640]{2,1,0:T(8,128)S(1)}, f32[3,80,640]{2,1,0:T(8,128)S(1)}, u32[]{:S(2)}, u32[]{:S(2)}) collective-permute-start(f32[3,80,640]{2,1,0:T(8,128)S(1)} %get-tuple-element.40), channel_id=1, source_target_pairs={{1,0},{2,1},{3,2},{4,3},{5,4},{6,5},{7,6},{9,8},{10,9},{11,10},{12... | collective-permute-start | bytes 1843208 | tf_op jit(solution)/shard_map/ppermute | solution.py:108
  17.4 35.6 %collective-permute-start = (f32[3,80,640]{2,1,0:T(8,128)S(1)}, f32[3,80,640]{2,1,0:T(8,128)S(1)}, u32[]{:S(2)}, u32[]{:S(2)}) collective-permute-start(f32[3,80,640]{2,1,0:T(8,128)S(1)} %get-tuple-element.41), channel_id=1, source_target_pairs={{0,1},{1,2},{2,3},{3,4},{4,5},{5,6},{6,7},{8,9},{9,10},{10,11},{11... | collective-permute-start | bytes 1843208 | tf_op jit(solution)/shard_map/ppermute | solution.py:108
  21.7 30.3 %collective-permute-start.3 = (f32[20,3,640]{2,1,0:T(4,128)S(1)}, f32[20,3,640]{2,1,0:T(4,128)S(1)}, u32[]{:S(2)}, u32[]{:S(2)}) collective-permute-start(f32[20,3,640]{2,1,0:T(4,128)S(1)} %get-tuple-element.38), channel_id=1, source_target_pairs={{8,0},{9,1},{10,2},{11,3},{12,4},{13,5},{14,6},{15,7},{16,8},{17,9... | collective-permute-start | bytes 460808 | tf_op jit(solution)/shard_map/ppermute | solution.py:108
  23.0 29.0 %collective-permute-start.6 = (f32[20,3,640]{2,1,0:T(4,128)S(1)}, f32[20,3,640]{2,1,0:T(4,128)S(1)}, u32[]{:S(2)}, u32[]{:S(2)}) collective-permute-start(f32[20,3,640]{2,1,0:T(4,128)S(1)} %get-tuple-element.39), channel_id=1, source_target_pairs={{0,8},{1,9},{2,10},{3,11},{4,12},{5,13},{6,14},{7,15},{8,16},{9,17... | collective-permute-start | bytes 460808 | tf_op jit(solution)/shard_map/ppermute | solution.py:108
  29.6 0.7 collective-permute-start.2
  30.3 0.7 collective-permute-start.7
  30.9 15.8 %collective-permute-start.5 = (f32[3,3,640]{2,1,0:T(4,128)S(1)}, f32[3,3,640]{2,1,0:T(4,128)S(1)}, u32[]{:S(2)}, u32[]{:S(2)}) collective-permute-start(f32[3,3,640]{2,1,0:T(4,128)S(1)} %get-tuple-element.36), channel_id=1, source_target_pairs={{0,9},{1,10},{2,11},{3,12},{4,13},{5,14},{6,15},{8,17},{9,18},{10,... | collective-permute-start | bytes 69128 | tf_op jit(solution)/shard_map/ppermute | solution.py:108
  46.7 5.3 %collective-permute-start.4 = (f32[3,3,640]{2,1,0:T(4,128)S(1)}, f32[3,3,640]{2,1,0:T(4,128)S(1)}, u32[]{:S(2)}, u32[]{:S(2)}) collective-permute-start(f32[3,3,640]{2,1,0:T(4,128)S(1)} %get-tuple-element.37), channel_id=1, source_target_pairs={{9,0},{10,1},{11,2},{12,3},{13,4},{14,5},{15,6},{17,8},{18,9},{19,... | collective-permute-start | bytes 69128 | tf_op jit(solution)/shard_map/ppermute | solution.py:108
  53.0 0.9 copy-start
  53.9 0.8 copy-start.2
  77.9 38.2 %collective-permute-start.9 = (f32[3,80,640]{2,1,0:T(8,128)S(1)}, f32[3,80,640]{2,1,0:T(8,128)S(1)}, u32[]{:S(2)}, u32[]{:S(2)}) collective-permute-start(f32[3,80,640]{2,1,0:T(8,128)S(1)} %get-tuple-element.32), channel_id=1, source_target_pairs={{1,0},{2,1},{3,2},{4,3},{5,4},{6,5},{7,6},{9,8},{10,9},{11,10},{12... | collective-permute-start | bytes 1843208 | tf_op jit(solution)/shard_map/ppermute | solution.py:108
  79.2 36.9 %collective-permute-start.8 = (f32[3,80,640]{2,1,0:T(8,128)S(1)}, f32[3,80,640]{2,1,0:T(8,128)S(1)}, u32[]{:S(2)}, u32[]{:S(2)}) collective-permute-start(f32[3,80,640]{2,1,0:T(8,128)S(1)} %get-tuple-element.33), channel_id=1, source_target_pairs={{0,1},{1,2},{2,3},{3,4},{4,5},{5,6},{6,7},{8,9},{9,10},{10,11},{11... | collective-permute-start | bytes 1843208 | tf_op jit(solution)/shard_map/ppermute | solution.py:108
  85.5 29.6 %collective-permute-start.11 = (f32[20,3,640]{2,1,0:T(4,128)S(1)}, f32[20,3,640]{2,1,0:T(4,128)S(1)}, u32[]{:S(2)}, u32[]{:S(2)}) collective-permute-start(f32[20,3,640]{2,1,0:T(4,128)S(1)} %get-tuple-element.30), channel_id=1, source_target_pairs={{8,0},{9,1},{10,2},{11,3},{12,4},{13,5},{14,6},{15,7},{16,8},{17,9... | collective-permute-start | bytes 460808 | tf_op jit(solution)/shard_map/ppermute | solution.py:108
  86.8 28.3 %collective-permute-start.14 = (f32[20,3,640]{2,1,0:T(4,128)S(1)}, f32[20,3,640]{2,1,0:T(4,128)S(1)}, u32[]{:S(2)}, u32[]{:S(2)}) collective-permute-start(f32[20,3,640]{2,1,0:T(4,128)S(1)} %get-tuple-element.31), channel_id=1, source_target_pairs={{0,8},{1,9},{2,10},{3,11},{4,12},{5,13},{6,14},{7,15},{8,16},{9,17... | collective-permute-start | bytes 460808 | tf_op jit(solution)/shard_map/ppermute | solution.py:108
  92.3 0.7 collective-permute-start.10
  93.0 0.7 collective-permute-start.15
  93.7 14.9 %collective-permute-start.13 = (f32[3,3,640]{2,1,0:T(4,128)S(1)}, f32[3,3,640]{2,1,0:T(4,128)S(1)}, u32[]{:S(2)}, u32[]{:S(2)}) collective-permute-start(f32[3,3,640]{2,1,0:T(4,128)S(1)} %get-tuple-element.28), channel_id=1, source_target_pairs={{0,9},{1,10},{2,11},{3,12},{4,13},{5,14},{6,15},{8,17},{9,18},{10,... | collective-permute-start | bytes 69128 | tf_op jit(solution)/shard_map/ppermute | solution.py:108
  108.6 6.4 %collective-permute-start.12 = (f32[3,3,640]{2,1,0:T(4,128)S(1)}, f32[3,3,640]{2,1,0:T(4,128)S(1)}, u32[]{:S(2)}, u32[]{:S(2)}) collective-permute-start(f32[3,3,640]{2,1,0:T(4,128)S(1)} %get-tuple-element.29), channel_id=1, source_target_pairs={{9,0},{10,1},{11,2},{12,3},{13,4},{14,5},{15,6},{17,8},{18,9},{19,... | collective-permute-start | bytes 69128 | tf_op jit(solution)/shard_map/ppermute | solution.py:108
  116.0 0.8 copy-start.3
  116.0 1.0 copy-start.5
  140.2 39.4 %collective-permute-start.17 = (f32[3,80,640]{2,1,0:T(8,128)S(1)}, f32[3,80,640]{2,1,0:T(8,128)S(1)}, u32[]{:S(2)}, u32[]{:S(2)}) collective-permute-start(f32[3,80,640]{2,1,0:T(8,128)S(1)} %get-tuple-element.24), channel_id=1, source_target_pairs={{1,0},{2,1},{3,2},{4,3},{5,4},{6,5},{7,6},{9,8},{10,9},{11,10},{12... | collective-permute-start | bytes 1843208 | tf_op jit(solution)/shard_map/ppermute | solution.py:108
  141.5 38.1 %collective-permute-start.16 = (f32[3,80,640]{2,1,0:T(8,128)S(1)}, f32[3,80,640]{2,1,0:T(8,128)S(1)}, u32[]{:S(2)}, u32[]{:S(2)}) collective-permute-start(f32[3,80,640]{2,1,0:T(8,128)S(1)} %get-tuple-element.25), channel_id=1, source_target_pairs={{0,1},{1,2},{2,3},{3,4},{4,5},{5,6},{6,7},{8,9},{9,10},{10,11},{11... | collective-permute-start | bytes 1843208 | tf_op jit(solution)/shard_map/ppermute | solution.py:108
  149.1 29.6 %collective-permute-start.19 = (f32[20,3,640]{2,1,0:T(4,128)S(1)}, f32[20,3,640]{2,1,0:T(4,128)S(1)}, u32[]{:S(2)}, u32[]{:S(2)}) collective-permute-start(f32[20,3,640]{2,1,0:T(4,128)S(1)} %get-tuple-element.22), channel_id=1, source_target_pairs={{8,0},{9,1},{10,2},{11,3},{12,4},{13,5},{14,6},{15,7},{16,8},{17,9... | collective-permute-start | bytes 460808 | tf_op jit(solution)/shard_map/ppermute | solution.py:108
  150.4 28.3 %collective-permute-start.22 = (f32[20,3,640]{2,1,0:T(4,128)S(1)}, f32[20,3,640]{2,1,0:T(4,128)S(1)}, u32[]{:S(2)}, u32[]{:S(2)}) collective-permute-start(f32[20,3,640]{2,1,0:T(4,128)S(1)} %get-tuple-element.23), channel_id=1, source_target_pairs={{0,8},{1,9},{2,10},{3,11},{4,12},{5,13},{6,14},{7,15},{8,16},{9,17... | collective-permute-start | bytes 460808 | tf_op jit(solution)/shard_map/ppermute | solution.py:108
  155.9 0.7 collective-permute-start.18
  156.6 0.7 collective-permute-start.23
  157.3 14.9 %collective-permute-start.21 = (f32[3,3,640]{2,1,0:T(4,128)S(1)}, f32[3,3,640]{2,1,0:T(4,128)S(1)}, u32[]{:S(2)}, u32[]{:S(2)}) collective-permute-start(f32[3,3,640]{2,1,0:T(4,128)S(1)} %get-tuple-element.20), channel_id=1, source_target_pairs={{0,9},{1,10},{2,11},{3,12},{4,13},{5,14},{6,15},{8,17},{9,18},{10,... | collective-permute-start | bytes 69128 | tf_op jit(solution)/shard_map/ppermute | solution.py:108
  172.2 6.5 %collective-permute-start.20 = (f32[3,3,640]{2,1,0:T(4,128)S(1)}, f32[3,3,640]{2,1,0:T(4,128)S(1)}, u32[]{:S(2)}, u32[]{:S(2)}) collective-permute-start(f32[3,3,640]{2,1,0:T(4,128)S(1)} %get-tuple-element.21), channel_id=1, source_target_pairs={{9,0},{10,1},{11,2},{12,3},{13,4},{14,5},{15,6},{17,8},{18,9},{19,... | collective-permute-start | bytes 69128 | tf_op jit(solution)/shard_map/ppermute | solution.py:108
  179.6 0.8 copy-start.1
  179.6 1.1 copy-start.4
  180.7 14.5 %copy-start.6 = (f32[8,128]{1,0:T(8,128)S(1)}, f32[8,128]{1,0:T(8,128)}, u32[]{:S(2)}) copy-start(f32[8,128]{1,0:T(8,128)} %get-tuple-element.15) | copy-start | bytes 12292
  180.7 14.5 %copy-start.7 = (f32[8,128]{1,0:T(8,128)S(1)}, f32[8,128]{1,0:T(8,128)}, u32[]{:S(2)}) copy-start(f32[8,128]{1,0:T(8,128)} %get-tuple-element.16) | copy-start | bytes 12292

commit v2 on v0

v2 whole, which is shorter than its diff:
```python
import functools

import jax
import jax.numpy as jnp
from jax import lax
from jax.experimental import pallas as pl
from jax.experimental.pallas import tpu as pltpu
from jax.sharding import PartitionSpec as P

RAD = 3
ITERS = 3
LANES = 128
ROWS = 8


def smear_x(row, taps):
    length = row.shape[1]
    padded = jnp.concatenate([row, jnp.zeros((row.shape[0], LANES), row.dtype)], axis=1)
    total = length + LANES
    result = taps[RAD] * row
    for k in range(2 * RAD + 1):
        if k != RAD:
            moved = pltpu.roll(padded, (RAD - k) % total, 1)
            result = result + taps[k] * moved[:, :length]
    return result


def smear_x_all(src, dst, taps):
    planes, height, _ = src.shape
    chunk = 2 * ROWS if height % (2 * ROWS) == 0 else ROWS

    def body(z, _):
        for y in range(0, height, chunk):
            dst[z, y : y + chunk, :] = smear_x(src[z, y : y + chunk, :], taps)
        return 0

    lax.fori_loop(0, planes, body, 0)


def first_kernel(kernel_ref, d_ref, u_ref):
    taps = [kernel_ref[2, k] for k in range(2 * RAD + 1)]
    smear_x_all(d_ref, u_ref, taps)


def smear_y(column, taps, height):
    result = taps[RAD] * column[:height]
    for k in range(2 * RAD + 1):
        if k != RAD:
            moved = pltpu.roll(column, (RAD - k) % (height + ROWS), 0)
            result = result + taps[k] * moved[:height]
    return result


def taps_of(kernel_ref, row):
    return [kernel_ref[row, k] for k in range(2 * RAD + 1)]


def rim_kernel(kernel_ref, u_ref, ylo_ref, yhi_ref, vtop_ref, vbot_ref, tail_ref):
    planes = tail_ref.shape[0]
    have, height, length = u_ref.shape
    ky = taps_of(kernel_ref, 0)

    def fill(z, _):
        tail_ref[z] = jnp.zeros((ROWS, length), tail_ref.dtype)
        tail_ref[z, 0:RAD, :] = yhi_ref[z]
        tail_ref[z, ROWS - RAD : ROWS, :] = ylo_ref[z]
        return 0

    lax.fori_loop(0, planes, fill, 0)
    for x in range(0, length, LANES):
        cols = slice(x, x + LANES)

        def body(i, _, cols=cols):
            for out, z, t in ((vtop_ref, i, i), (vbot_ref, have - RAD + i, planes - RAD + i)):
                column = jnp.concatenate([u_ref[z, :, cols], tail_ref[t, :, cols]], axis=0)
                out[i, :, cols] = smear_y(column, ky, height)
            return 0

        lax.fori_loop(0, RAD, body, 0)


def finish(v_ref, z, cols, kz, p_ref, pz, d_ref, out_ref, to, dev_ref):
    height = p_ref.shape[1]
    b = kz[0] * v_ref[z, :, cols]
    for k in range(1, 2 * RAD + 1):
        b = b + kz[k] * v_ref[z + k, :, cols]
    p = p_ref[pz, :, cols]
    if d_ref is None:
        out_ref[to, :, cols] = p / b
    else:
        out_ref[to, :, cols] = p / (b * d_ref[0][d_ref[1], :, cols])
    off = jnp.max(jnp.abs(b - 1.0).reshape(height // ROWS, ROWS, LANES), axis=0)
    dev_ref[...] = jnp.maximum(dev_ref[...], off)


def smear_planes(src, dst, taps, begin, count):
    height = src.shape[1]
    chunk = 2 * ROWS if height % (2 * ROWS) == 0 else ROWS

    def body(z, _):
        for y in range(0, height, chunk):
            dst[z, y : y + chunk, :] = smear_x(src[z, y : y + chunk, :], taps)
        return 0

    lax.fori_loop(begin, begin + count, body, 0)


def inner_kernel(last, *refs):
    if last:
        kernel_ref, p_ref, u_ref, tail_ref, vtop_ref, vbot_ref, d_ref, out_ref, dev_ref, below_ref, above_ref, v = refs
    else:
        kernel_ref, p_ref, u_ref, tail_ref, vtop_ref, vbot_ref, out_ref, unext_ref, dev_ref, below_ref, above_ref, v = refs
        d_ref = None
    planes, height, length = p_ref.shape
    ky = taps_of(kernel_ref, 0)
    kz = taps_of(kernel_ref, 1)
    dev_ref[...] = jnp.zeros_like(dev_ref)
    for z in range(RAD):
        v[z] = vtop_ref[z]
        v[planes - RAD + z] = vbot_ref[z]
    for x in range(0, length, LANES):
        cols = slice(x, x + LANES)

        def smear(z, _, cols=cols):
            column = jnp.concatenate([u_ref[z, :, cols], tail_ref[z, :, cols]], axis=0)
            v[z, :, cols] = smear_y(column, ky, height)
            return 0

        lax.fori_loop(RAD, planes - RAD, smear, 0)

        def body(z, _, cols=cols):
            d_at = None if d_ref is None else (d_ref, z + RAD)
            finish(v, z, cols, kz, p_ref, z + RAD, d_at, out_ref, z + RAD, dev_ref)
            return 0

        lax.fori_loop(0, planes - 2 * RAD, body, 0)
    for z in range(RAD):
        below_ref[z] = v[RAD + z]
        above_ref[z] = v[planes - 2 * RAD + z]
    if not last:
        smear_planes(out_ref, unext_ref, taps_of(kernel_ref, 2), RAD, planes - 2 * RAD)


def edge_kernel(last, *refs):
    kernel_ref, p_ref, zlo_ref, zhi_ref, vtop_ref, vbot_ref, below_ref, above_ref = refs[:8]
    d_ref = None
    if last:
        d_ref, _, whole_ref, dev_ref, v, out_ref, sems = refs[8:]
    else:
        out_ref, unext_ref, dev_ref, v = refs[8:]
    have, height, length = p_ref.shape
    kz = taps_of(kernel_ref, 1)
    dev_ref[...] = jnp.zeros_like(dev_ref)
    copies = []
    for side, parts in enumerate(((zlo_ref, vtop_ref, below_ref), (above_ref, vbot_ref, zhi_ref))):
        p_first = side * (have - RAD)
        first = side * RAD
        d_first = None if d_ref is None else side * (d_ref.shape[0] - RAD)
        for n, part in enumerate(parts):
            for z in range(RAD):
                v[n * RAD + z] = part[z]
        for x in range(0, length, LANES):
            cols = slice(x, x + LANES)

            def body(z, _, cols=cols, p_first=p_first, first=first, d_first=d_first):
                d_at = None if d_ref is None else (d_ref, d_first + z)
                finish(v, z, cols, kz, p_ref, p_first + z, d_at, out_ref, first + z, dev_ref)
                return 0

            lax.fori_loop(0, RAD, body, 0)
        if last:
            copy = pltpu.make_async_copy(
                out_ref.at[pl.ds(first, RAD)], whole_ref.at[pl.ds(d_first, RAD)], sems.at[side]
            )
            copy.start()
            copies.append(copy)
        else:
            smear_planes(out_ref, unext_ref, taps_of(kernel_ref, 2), first, RAD)
    for copy in copies:
        copy.wait()


def from_neighbour(block, axis, step):
    count = lax.axis_size(axis)
    pairs = [(i + step, i) for i in range(count) if 0 <= i + step < count]
    return lax.ppermute(block, axis, pairs)


def max_over(value, axis):
    count = lax.axis_size(axis)
    step = 1
    while step < count:
        value = jnp.maximum(value, lax.ppermute(value, axis, [(i, (i + step) % count) for i in range(count)]))
        step *= 2
    return value


def shards(data_weight, blob_taps):
    kernel = blob_taps / jnp.sum(blob_taps, axis=1, keepdims=True)
    d = jnp.transpose(data_weight, (1, 0, 2))
    planes, height, length = d.shape
    vmem = pl.BlockSpec(memory_space=pltpu.VMEM)
    smem = pl.BlockSpec(memory_space=pltpu.SMEM)
    whole = jax.ShapeDtypeStruct(d.shape, d.dtype)
    rim = jax.ShapeDtypeStruct((RAD, height, length), d.dtype)
    tails = jax.ShapeDtypeStruct((planes, ROWS, length), d.dtype)
    dev_shape = jax.ShapeDtypeStruct((ROWS, LANES), d.dtype)
    params = pltpu.CompilerParams(vmem_limit_bytes=22 * 1024 * 1024)

    anywhere = pl.BlockSpec(memory_space=pl.ANY)
    rims = jax.ShapeDtypeStruct((2 * RAD, height, length), d.dtype)

    def call(body, outs, args, scratch=(), name=None, last_any=False):
        in_specs = [smem] + [vmem] * len(args)
        out_specs = [vmem] * len(outs)
        aliases = {}
        if last_any:
            in_specs[-1] = out_specs[0] = anywhere
            aliases = {len(args): 0}
        return pl.pallas_call(
            body,
            out_shape=outs,
            in_specs=in_specs,
            out_specs=out_specs,
            scratch_shapes=scratch,
            input_output_aliases=aliases,
            compiler_params=params,
            name=name,
        )(kernel, *args)

    (u,) = call(first_kernel, [whole], [d], name="first")
    p = p_rims = d
    u_rims = u
    devs = []
    full_v = [pltpu.VMEM(d.shape, d.dtype)]
    edge_v = [pltpu.VMEM((3 * RAD, height, length), d.dtype)]
    for iteration in range(ITERS):
        last = iteration == ITERS - 1
        if iteration == 0:
            yend, yfirst = u[:, height - RAD :], u[:, :RAD]
        else:
            parts = (u_rims[:RAD], u[RAD : planes - RAD], u_rims[RAD:])
            yend = jnp.concatenate([part[:, height - RAD :] for part in parts], axis=0)
            yfirst = jnp.concatenate([part[:, :RAD] for part in parts], axis=0)
        ylo = from_neighbour(yend, "gy", -1)
        yhi = from_neighbour(yfirst, "gy", 1)
        vtop, vbot, tail = call(rim_kernel, [rim, rim, tails], [u_rims, ylo, yhi], name="rim")
        zlo = from_neighbour(vbot, "gz", -1)
        zhi = from_neighbour(vtop, "gz", 1)
        state = [whole] if last else [whole, whole]
        extra = [d] if last else []
        outs = call(
            functools.partial(inner_kernel, last),
            state + [dev_shape, rim, rim],
            [p, u, tail, vtop, vbot] + extra,
            full_v,
            name="inner",
        )
        fresh, (dev, below, above) = outs[: len(state)], outs[len(state) :]
        args = [p_rims, zlo, zhi, vtop, vbot, below, above]
        if last:
            scratch = edge_v + [pltpu.VMEM(rims.shape, d.dtype), pltpu.SemaphoreType.DMA((2,))]
            weight, edge_dev = call(
                functools.partial(edge_kernel, True), [whole, dev_shape], args + [d, fresh[0]], scratch, "edge", True
            )
        else:
            p, u = fresh
            p_rims, u_rims, edge_dev = call(
                functools.partial(edge_kernel, False), [rims, rims, dev_shape], args, edge_v, "edge"
            )
        devs.append(jnp.maximum(dev, edge_dev))
    local = jnp.max(jnp.stack(devs), axis=(1, 2))
    return jnp.transpose(weight, (1, 0, 2)), max_over(max_over(local, "gz"), "gy")


def solution(mesh):
    return jax.shard_map(
        shards,
        mesh=mesh,
        in_specs=(P("gy", "gz", None), P()),
        out_specs=(P("gy", "gz", None), P()),
        check_vma=False,
    )
```

time: 280 us -> 138 us (0.49)
  other arithmetic: 151 us -> 2.38 us
  Pallas kernels: 0 us -> 55.5 us
  blocking collectives: 45.7 us -> 0 us
  waiting for transfers between devices: 32.6 us -> 26.7 us
  starting transfers between devices: 45 us -> 49.3 us
    add x6 -> x0, other arithmetic: 88 us -> none  [smear_valid(): result + kernel[offset] * lax.slice_in_dim(padded, offset, offset + lengt...]
    pallas_call x0 -> x10, Pallas kernels: none -> 55.5 us  [call(): pl.pallas_call(body, out_shape=outs, in_specs=in_specs, out_specs=out_spe...]
    pmax x1 -> x0, blocking collectives: 45.7 us -> none  [shards(): changes.append(lax.pmax(deviation, ('gy', 'gz')))]
    reduce_max x3 -> x1, other arithmetic: 45.7 us -> 0.11 us  [shards(): local = jnp.max(jnp.stack(devs), axis=(1, 2))]
    mul x2 -> x0, other arithmetic: 8.77 us -> none  [shards(): product = weight * data_weight]
    ppermute x12 -> x17, waiting for transfers between devices: 32.6 us -> 26.7 us  [the longest x12 13.6 us: from_neighbour(): return lax.ppermute(block, axis, pairs)]
    div x1 -> x0, other arithmetic: 4.68 us -> none  [shards(): weight = weight / blurred]
    ppermute x12 -> x17, starting transfers between devices: 45 us -> 49.3 us  [the longest x12 34.9 us: from_neighbour(): return lax.ppermute(block, axis, pairs)]
  transfers between devices with their start and end apart: 12 -> 17, of which waited for: 11 -> 11; matrix products, arithmetic and copies ran while one was open for 0% -> 0% of each run, Pallas kernels for 0% -> 22%
where the time goes in v2:
time: 138 us; the launch traced here: 137 us
  Pallas kernels  55.5 us (40%)
  starting transfers between devices  49.3 us (36%)
  waiting for transfers between devices  26.7 us (19%)
  local copies, waits for them, and re-layouts  2.4 us (2%)
  other arithmetic  2.38 us (2%)
    pallas_call x10, Pallas kernels, call(): pl.pallas_call(body, out_shape=outs, in_specs=in_specs, out_specs=out_spe...  55.5 us
    ppermute x12, starting transfers between devices, from_neighbour(): return lax.ppermute(block, axis, pairs)  34.9 us
    ppermute x5, starting transfers between devices, max_over(): lax.ppermute(value, axis, [(i, (i + step) % count) for i in range(count)])  14.4 us
    ppermute x12, waiting for transfers between devices, from_neighbour(): return lax.ppermute(block, axis, pairs)  13.6 us
    ppermute x5, waiting for transfers between devices, max_over(): lax.ppermute(value, axis, [(i, (i + step) % count) for i in range(count)])  13 us
  transfers between devices with their start and end apart: 17, of which 11 were waited for; matrix products, arithmetic and copies ran while one was open for 0% of the time, Pallas kernels for 22%

profile of v2, /device:TPU:0, one launch (start us, length us, event | category | flops | bytes accessed | tf_op | source)
XLA Modules:
  0.0 137.2 jit_solution(9204343665861029532)
XLA Ops:
  0.6 0.8 reduce_sum.9
  1.4 0.8 broadcast_divide_fusion.kernel_ref.refs_0_
  2.2 0.0 copy-start
  2.2 2.2 %copy-done = f32[80,20,640]{2,0,1:T(8,128)S(1)} copy-done((f32[80,20,640]{2,0,1:T(8,128)S(1)}, f32[80,20,640]{2,0,1:T(8,128)}, u32[]{:S(2)}) %copy-start) | copy-done | bytes 4096024
  4.3 8.4 %first.1.u_ref.refs_2_ = f32[20,80,640]{2,1,0:T(8,128)S(1)} custom-call(f32[3,7]{1,0:T(4,128)S(1)} %broadcast_divide_fusion.kernel_ref.refs_0_, f32[20,80,640]{2,1,0:T(8,128)S(1)} %bitcast.8), custom_call_target="tpu_custom_call" | custom-call | tf_op jit(solution)/shard_map/first/pallas_call | solution.py:220
  12.8 0.0 copy-start.1
  12.8 0.1 fusion.2
  12.9 5.2 %collective-permute-start = (f32[20,3,640]{2,1,0:T(4,128)S(1)}, f32[20,3,640]{2,1,0:T(4,128)S(1)}, u32[]{:S(2)}, u32[]{:S(2)}) collective-permute-start(f32[20,3,640]{2,1,0:T(4,128)S(1)} %get-tuple-element.69), channel_id=1, source_target_pairs={{0,8},{8,16},{16,24},{1,9},{9,17},{17,25},{2,10},{10,18},{18,26},{... | collective-permute-start | bytes 460808 | tf_op jit(solution)/shard_map/ppermute | solution.py:186
  18.1 1.3 collective-permute-start.1
  19.4 3.0 %collective-permute-done.ylo_ref = f32[20,3,640]{2,1,0:T(4,128)S(1)} collective-permute-done((f32[20,3,640]{2,1,0:T(4,128)S(1)}, f32[20,3,640]{2,1,0:T(4,128)S(1)}, u32[]{:S(2)}, u32[]{:S(2)}) %collective-permute-start) | collective-permute-done | bytes 153632 | tf_op jit(solution)/shard_map/ppermute | solution.py:186
  22.4 4.1 %collective-permute-done.1.yhi_ref = f32[20,3,640]{2,1,0:T(4,128)S(1)} collective-permute-done((f32[20,3,640]{2,1,0:T(4,128)S(1)}, f32[20,3,640]{2,1,0:T(4,128)S(1)}, u32[]{:S(2)}, u32[]{:S(2)}) %collective-permute-start.1) | collective-permute-done | bytes 153632 | tf_op jit(solution)/shard_map/ppermute | solution.py:186
  26.6 1.8 %rim.3 = (f32[3,80,640]{2,1,0:T(8,128)S(1)}, f32[3,80,640]{2,1,0:T(8,128)S(1)}, f32[20,8,640]{2,1,0:T(8,128)S(1)}) custom-call(f32[3,7]{1,0:T(4,128)S(1)} %broadcast_divide_fusion.kernel_ref.refs_0_, f32[20,80,640]{2,1,0:T(8,128)S(1)} %first.1.u_ref.refs_2_, f32[20,3,640]{2,1,0:T(4,128)S(1)} %collective-permute-done.ylo_ref, ...), custom_call_target="tpu_custom_call" | custom-call | tf_op jit(solution)/shard_map/rim/pallas_call | solution.py:220
  28.4 1.3 collective-permute-start.2
  29.7 1.3 collective-permute-start.3
  31.0 0.0 copy-done.1
  31.0 11.3 %inner.3 = (f32[20,80,640]{2,1,0:T(8,128)S(1)}, f32[20,80,640]{2,1,0:T(8,128)S(1)}, f32[8,128]{1,0:T(8,128)S(1)}, f32[3,80,640]{2,1,0:T(8,128)S(1)}, f32[3,80,640]{2,1,0:T(8,128)S(1)}) custom-call(f32[3,7]{1,0:T(4,128)S(1)} %broadcast_divide_fusion.kernel_ref.refs_0_, f32[20,80,640]{2,1,0:T(8,128)S(1)} %bitcast.9, f32[20,80,640]{2,1,0:T(8,128)S(1)} %first.1.u_ref.refs_2_, ...), custom_call_target="tpu_custom_call" | custom-call | tf_op jit(solution)/shard_map/inner/pallas_call | solution.py:220
  42.4 0.1 fusion.1
  42.4 0.0 collective-permute-done.2.refs_2_
  42.5 0.0 collective-permute-done.3.refs_3_
  42.5 4.2 %edge.3 = (f32[6,80,640]{2,1,0:T(8,128)S(1)}, f32[6,80,640]{2,1,0:T(8,128)S(1)}, f32[8,128]{1,0:T(8,128)S(1)}) custom-call(f32[3,7]{1,0:T(4,128)S(1)} %broadcast_divide_fusion.kernel_ref.refs_0_, f32[20,80,640]{2,1,0:T(8,128)S(1)} %bitcast.10, f32[3,80,640]{2,1,0:T(8,128)S(1)} %collective-permute-done.2.refs_2_, ...), custom_call_target="tpu_custom_call" | custom-call | tf_op jit(solution)/shard_map/edge/pallas_call | solution.py:220
  46.7 1.3 collective-permute-start.5
  48.1 4.6 %collective-permute-start.4 = (f32[20,3,640]{2,1,0:T(4,128)S(1)}, f32[20,3,640]{2,1,0:T(4,128)S(1)}, u32[]{:S(2)}, u32[]{:S(2)}) collective-permute-start(f32[20,3,640]{2,1,0:T(4,128)S(1)} %pad_maximum_fusion), channel_id=1, source_target_pairs={{0,8},{8,16},{16,24},{1,9},{9,17},{17,25},{2,10},{10,18},{18,26},{... | collective-permute-start | bytes 460808 | tf_op jit(solution)/shard_map/ppermute | solution.py:186
  52.6 1.7 %collective-permute-done.5.yhi_ref = f32[20,3,640]{2,1,0:T(4,128)S(1)} collective-permute-done((f32[20,3,640]{2,1,0:T(4,128)S(1)}, f32[20,3,640]{2,1,0:T(4,128)S(1)}, u32[]{:S(2)}, u32[]{:S(2)}) %collective-permute-start.5) | collective-permute-done | bytes 153632 | tf_op jit(solution)/shard_map/ppermute | solution.py:186
  54.4 1.5 %collective-permute-done.4.ylo_ref = f32[20,3,640]{2,1,0:T(4,128)S(1)} collective-permute-done((f32[20,3,640]{2,1,0:T(4,128)S(1)}, f32[20,3,640]{2,1,0:T(4,128)S(1)}, u32[]{:S(2)}, u32[]{:S(2)}) %collective-permute-start.4) | collective-permute-done | bytes 153632 | tf_op jit(solution)/shard_map/ppermute | solution.py:186
  55.9 1.8 %rim.4 = (f32[3,80,640]{2,1,0:T(8,128)S(1)}, f32[3,80,640]{2,1,0:T(8,128)S(1)}, f32[20,8,640]{2,1,0:T(8,128)S(1)}) custom-call(f32[3,7]{1,0:T(4,128)S(1)} %broadcast_divide_fusion.kernel_ref.refs_0_, f32[6,80,640]{2,1,0:T(8,128)S(1)} %get-tuple-element.39.u_ref, f32[20,3,640]{2,1,0:T(4,128)S(1)} %collective-permute-done.4.ylo_ref, ...), custom_call_target="tpu_custom_call" | custom-call | tf_op jit(solution)/shard_map/rim/pallas_call | solution.py:220
  57.7 5.6 %collective-permute-start.6 = (f32[3,80,640]{2,1,0:T(8,128)S(1)}, f32[3,80,640]{2,1,0:T(8,128)S(1)}, u32[]{:S(2)}, u32[]{:S(2)}) collective-permute-start(f32[3,80,640]{2,1,0:T(8,128)S(1)} %get-tuple-element.41.refs_5_), channel_id=1, source_target_pairs={{0,1},{1,2},{2,3},{3,4},{4,5},{5,6},{6,7},{8,9},{9,10},{10,11},{11... | collective-permute-start | bytes 1843208 | tf_op jit(solution)/shard_map/ppermute | solution.py:186
  63.3 1.3 collective-permute-start.7
  64.6 11.3 %inner.4 = (f32[20,80,640]{2,1,0:T(8,128)S(1)}, f32[20,80,640]{2,1,0:T(8,128)S(1)}, f32[8,128]{1,0:T(8,128)S(1)}, f32[3,80,640]{2,1,0:T(8,128)S(1)}, f32[3,80,640]{2,1,0:T(8,128)S(1)}) custom-call(f32[3,7]{1,0:T(4,128)S(1)} %broadcast_divide_fusion.kernel_ref.refs_0_, f32[20,80,640]{2,1,0:T(8,128)S(1)} %get-tuple-element.43.refs_1_, ...), custom_call_target="tpu_custom_call" | custom-call | tf_op jit(solution)/shard_map/inner/pallas_call | solution.py:220
  75.9 0.1 fusion
  76.0 0.0 collective-permute-done.6.refs_2_
  76.0 0.0 collective-permute-done.7.refs_3_
  76.0 4.2 %edge.4 = (f32[6,80,640]{2,1,0:T(8,128)S(1)}, f32[6,80,640]{2,1,0:T(8,128)S(1)}, f32[8,128]{1,0:T(8,128)S(1)}) custom-call(f32[3,7]{1,0:T(4,128)S(1)} %broadcast_divide_fusion.kernel_ref.refs_0_, f32[6,80,640]{2,1,0:T(8,128)S(1)} %get-tuple-element.38.refs_1_, f32[3,80,640]{2,1,0:T(8,128)S(1)} %collective-permute-done.6.refs_2_, ...), custom_call_target="tpu_custom_call" | custom-call | tf_op jit(solution)/shard_map/edge/pallas_call | solution.py:220
  80.3 1.3 collective-permute-start.9
  81.7 4.7 %collective-permute-start.8 = (f32[20,3,640]{2,1,0:T(4,128)S(1)}, f32[20,3,640]{2,1,0:T(4,128)S(1)}, u32[]{:S(2)}, u32[]{:S(2)}) collective-permute-start(f32[20,3,640]{2,1,0:T(4,128)S(1)} %pad_maximum_fusion.2), channel_id=1, source_target_pairs={{0,8},{8,16},{16,24},{1,9},{9,17},{17,25},{2,10},{10,18},{18,26},{... | collective-permute-start | bytes 460808 | tf_op jit(solution)/shard_map/ppermute | solution.py:186
  86.4 1.7 %collective-permute-done.9.yhi_ref = f32[20,3,640]{2,1,0:T(4,128)S(1)} collective-permute-done((f32[20,3,640]{2,1,0:T(4,128)S(1)}, f32[20,3,640]{2,1,0:T(4,128)S(1)}, u32[]{:S(2)}, u32[]{:S(2)}) %collective-permute-start.9) | collective-permute-done | bytes 153632 | tf_op jit(solution)/shard_map/ppermute | solution.py:186
  88.1 1.5 %collective-permute-done.8.ylo_ref = f32[20,3,640]{2,1,0:T(4,128)S(1)} collective-permute-done((f32[20,3,640]{2,1,0:T(4,128)S(1)}, f32[20,3,640]{2,1,0:T(4,128)S(1)}, u32[]{:S(2)}, u32[]{:S(2)}) %collective-permute-start.8) | collective-permute-done | bytes 153632 | tf_op jit(solution)/shard_map/ppermute | solution.py:186
  89.6 1.8 %rim.5 = (f32[3,80,640]{2,1,0:T(8,128)S(1)}, f32[3,80,640]{2,1,0:T(8,128)S(1)}, f32[20,8,640]{2,1,0:T(8,128)S(1)}) custom-call(f32[3,7]{1,0:T(4,128)S(1)} %broadcast_divide_fusion.kernel_ref.refs_0_, f32[6,80,640]{2,1,0:T(8,128)S(1)} %get-tuple-element.48.u_ref, f32[20,3,640]{2,1,0:T(4,128)S(1)} %collective-permute-done.8.ylo_ref, ...), custom_call_target="tpu_custom_call" | custom-call | tf_op jit(solution)/shard_map/rim/pallas_call | solution.py:220
  91.5 5.8 %collective-permute-start.10 = (f32[3,80,640]{2,1,0:T(8,128)S(1)}, f32[3,80,640]{2,1,0:T(8,128)S(1)}, u32[]{:S(2)}, u32[]{:S(2)}) collective-permute-start(f32[3,80,640]{2,1,0:T(8,128)S(1)} %get-tuple-element.50.refs_5_), channel_id=1, source_target_pairs={{0,1},{1,2},{2,3},{3,4},{4,5},{5,6},{6,7},{8,9},{9,10},{10,11},{11... | collective-permute-start | bytes 1843208 | tf_op jit(solution)/shard_map/ppermute | solution.py:186
  97.2 1.3 collective-permute-start.11
  98.6 7.9 %inner.5 = (f32[20,80,640]{2,1,0:T(8,128)}, f32[8,128]{1,0:T(8,128)S(1)}, f32[3,80,640]{2,1,0:T(8,128)S(1)}, f32[3,80,640]{2,1,0:T(8,128)S(1)}) custom-call(f32[3,7]{1,0:T(4,128)S(1)} %broadcast_divide_fusion.kernel_ref.refs_0_, f32[20,80,640]{2,1,0:T(8,128)S(1)} %get-tuple-element.52.refs_1_, f32[20,80,640]{2,1,0:T(8,128)S(1)} %get-tuple-element.49.refs_2_, ...), custom_call_target="tpu_custom_call" | custom-call | tf_op jit(solution)/shard_map/inner/pallas_call | solution.py:220
  106.4 0.0 collective-permute-done.10.refs_2_
  106.4 0.0 collective-permute-done.11.refs_3_
  106.4 2.7 %edge.5 = (f32[20,80,640]{2,1,0:T(8,128)}, f32[8,128]{1,0:T(8,128)S(1)}) custom-call(f32[3,7]{1,0:T(4,128)S(1)} %broadcast_divide_fusion.kernel_ref.refs_0_, f32[6,80,640]{2,1,0:T(8,128)S(1)} %get-tuple-element.47.refs_1_, f32[3,80,640]{2,1,0:T(8,128)S(1)} %collective-permute-done.10.refs_2_, ...), custom_call_target="tpu_custom_call", output_to_operand_aliasing={{0}: (9, {})} | custom-call | tf_op jit(solution)/shard_map/edge/pallas_call | solution.py:220
  109.2 0.1 maximum_reduce_fusion
  109.3 7.6 %collective-permute-start.12 = (f32[3]{0:T(128)S(1)}, f32[3]{0:T(128)S(1)}, u32[]{:S(2)}, u32[]{:S(2)}) collective-permute-start(f32[3]{0:T(128)S(1)} %maximum_reduce_fusion), channel_id=1, source_target_pairs={{0,1},{1,2},{2,3},{3,4},{4,5},{5,6},{6,7},{7,0},{8,9},{9,10},{10,1... | collective-permute-start | bytes 44 | tf_op jit(solution)/shard_map/ppermute | solution.py:193
  116.9 0.8 collective-permute-done.12
  117.7 2.1 %collective-permute-start.13 = (f32[3]{0:T(128)S(1)}, f32[3]{0:T(128)S(1)}, u32[]{:S(2)}, u32[]{:S(2)}) collective-permute-start(f32[3]{0:T(128)S(1)} %max.27), channel_id=1, source_target_pairs={{0,2},{1,3},{2,4},{3,5},{4,6},{5,7},{6,0},{7,1},{8,10},{9,11},{10,... | collective-permute-start | bytes 44 | tf_op jit(solution)/shard_map/ppermute | solution.py:193
  119.8 2.4 %collective-permute-done.13 = f32[3]{0:T(128)S(1)} collective-permute-done((f32[3]{0:T(128)S(1)}, f32[3]{0:T(128)S(1)}, u32[]{:S(2)}, u32[]{:S(2)}) %collective-permute-start.13) | collective-permute-done | bytes 44 | tf_op jit(solution)/shard_map/ppermute | solution.py:193
  122.2 1.2 collective-permute-start.14
  123.4 2.3 %collective-permute-done.14 = f32[3]{0:T(128)S(1)} collective-permute-done((f32[3]{0:T(128)S(1)}, f32[3]{0:T(128)S(1)}, u32[]{:S(2)}, u32[]{:S(2)}) %collective-permute-start.14) | collective-permute-done | bytes 44 | tf_op jit(solution)/shard_map/ppermute | solution.py:193
  125.8 2.5 %collective-permute-start.15 = (f32[3]{0:T(128)S(1)}, f32[3]{0:T(128)S(1)}, u32[]{:S(2)}, u32[]{:S(2)}) collective-permute-start(f32[3]{0:T(128)S(1)} %max.29), channel_id=1, source_target_pairs={{0,8},{8,16},{16,24},{24,0},{1,9},{9,17},{17,25},{25,1},{2,10},{10... | collective-permute-start | bytes 44 | tf_op jit(solution)/shard_map/ppermute | solution.py:193
  128.2 4.0 %collective-permute-done.15 = f32[3]{0:T(128)S(1)} collective-permute-done((f32[3]{0:T(128)S(1)}, f32[3]{0:T(128)S(1)}, u32[]{:S(2)}, u32[]{:S(2)}) %collective-permute-start.15) | collective-permute-done | bytes 44 | tf_op jit(solution)/shard_map/ppermute | solution.py:193
  132.3 1.0 collective-permute-start.16
  133.3 3.5 %collective-permute-done.16 = f32[3]{0:T(128)S(1)} collective-permute-done((f32[3]{0:T(128)S(1)}, f32[3]{0:T(128)S(1)}, u32[]{:S(2)}, u32[]{:S(2)}) %collective-permute-start.16) | collective-permute-done | bytes 44 | tf_op jit(solution)/shard_map/ppermute | solution.py:193
  136.7 0.5 max.31
  (12 shorter events, 0.3 us)
Async XLA Ops:
  2.2 2.2 %copy-start = (f32[80,20,640]{2,0,1:T(8,128)S(1)}, f32[80,20,640]{2,0,1:T(8,128)}, u32[]{:S(2)}) copy-start(f32[80,20,640]{2,0,1:T(8,128)} %param.2) | copy-start | bytes 12288004
  12.8 18.2 %copy-start.1 = (f32[80,20,640]{2,0,1:T(8,128)S(1)}, f32[80,20,640]{2,0,1:T(8,128)}, u32[]{:S(2)}) copy-start(f32[80,20,640]{2,0,1:T(8,128)} %param.2) | copy-start | bytes 12288004
  12.9 9.5 %collective-permute-start = (f32[20,3,640]{2,1,0:T(4,128)S(1)}, f32[20,3,640]{2,1,0:T(4,128)S(1)}, u32[]{:S(2)}, u32[]{:S(2)}) collective-permute-start(f32[20,3,640]{2,1,0:T(4,128)S(1)} %get-tuple-element.69), channel_id=1, source_target_pairs={{0,8},{8,16},{16,24},{1,9},{9,17},{17,25},{2,10},{10,18},{18,26},{... | collective-permute-start | bytes 460808 | tf_op jit(solution)/shard_map/ppermute | solution.py:186
  18.1 8.4 %collective-permute-start.1 = (f32[20,3,640]{2,1,0:T(4,128)S(1)}, f32[20,3,640]{2,1,0:T(4,128)S(1)}, u32[]{:S(2)}, u32[]{:S(2)}) collective-permute-start(f32[20,3,640]{2,1,0:T(4,128)S(1)} %get-tuple-element.68), channel_id=1, source_target_pairs={{8,0},{16,8},{24,16},{9,1},{17,9},{25,17},{10,2},{18,10},{26,18},{... | collective-permute-start | bytes 460808 | tf_op jit(solution)/shard_map/ppermute | solution.py:186
  28.4 14.1 %collective-permute-start.2 = (f32[3,80,640]{2,1,0:T(8,128)S(1)}, f32[3,80,640]{2,1,0:T(8,128)S(1)}, u32[]{:S(2)}, u32[]{:S(2)}) collective-permute-start(f32[3,80,640]{2,1,0:T(8,128)S(1)} %get-tuple-element.33.refs_5_), channel_id=1, source_target_pairs={{0,1},{1,2},{2,3},{3,4},{4,5},{5,6},{6,7},{8,9},{9,10},{10,11},{11... | collective-permute-start | bytes 1843208 | tf_op jit(solution)/shard_map/ppermute | solution.py:186
  29.7 12.7 %collective-permute-start.3 = (f32[3,80,640]{2,1,0:T(8,128)S(1)}, f32[3,80,640]{2,1,0:T(8,128)S(1)}, u32[]{:S(2)}, u32[]{:S(2)}) collective-permute-start(f32[3,80,640]{2,1,0:T(8,128)S(1)} %get-tuple-element.34.refs_4_), channel_id=1, source_target_pairs={{1,0},{2,1},{3,2},{4,3},{5,4},{6,5},{7,6},{9,8},{10,9},{11,10},{12... | collective-permute-start | bytes 1843208 | tf_op jit(solution)/shard_map/ppermute | solution.py:186
  46.7 7.7 %collective-permute-start.5 = (f32[20,3,640]{2,1,0:T(4,128)S(1)}, f32[20,3,640]{2,1,0:T(4,128)S(1)}, u32[]{:S(2)}, u32[]{:S(2)}) collective-permute-start(f32[20,3,640]{2,1,0:T(4,128)S(1)} %pad_maximum_fusion.1), channel_id=1, source_target_pairs={{8,0},{16,8},{24,16},{9,1},{17,9},{25,17},{10,2},{18,10},{26,18},{... | collective-permute-start | bytes 460808 | tf_op jit(solution)/shard_map/ppermute | solution.py:186
  48.1 7.8 %collective-permute-start.4 = (f32[20,3,640]{2,1,0:T(4,128)S(1)}, f32[20,3,640]{2,1,0:T(4,128)S(1)}, u32[]{:S(2)}, u32[]{:S(2)}) collective-permute-start(f32[20,3,640]{2,1,0:T(4,128)S(1)} %pad_maximum_fusion), channel_id=1, source_target_pairs={{0,8},{8,16},{16,24},{1,9},{9,17},{17,25},{2,10},{10,18},{18,26},{... | collective-permute-start | bytes 460808 | tf_op jit(solution)/shard_map/ppermute | solution.py:186
  57.7 18.3 %collective-permute-start.6 = (f32[3,80,640]{2,1,0:T(8,128)S(1)}, f32[3,80,640]{2,1,0:T(8,128)S(1)}, u32[]{:S(2)}, u32[]{:S(2)}) collective-permute-start(f32[3,80,640]{2,1,0:T(8,128)S(1)} %get-tuple-element.41.refs_5_), channel_id=1, source_target_pairs={{0,1},{1,2},{2,3},{3,4},{4,5},{5,6},{6,7},{8,9},{9,10},{10,11},{11... | collective-permute-start | bytes 1843208 | tf_op jit(solution)/shard_map/ppermute | solution.py:186
  63.3 12.7 %collective-permute-start.7 = (f32[3,80,640]{2,1,0:T(8,128)S(1)}, f32[3,80,640]{2,1,0:T(8,128)S(1)}, u32[]{:S(2)}, u32[]{:S(2)}) collective-permute-start(f32[3,80,640]{2,1,0:T(8,128)S(1)} %get-tuple-element.42.refs_4_), channel_id=1, source_target_pairs={{1,0},{2,1},{3,2},{4,3},{5,4},{6,5},{7,6},{9,8},{10,9},{11,10},{12... | collective-permute-start | bytes 1843208 | tf_op jit(solution)/shard_map/ppermute | solution.py:186
  80.3 7.8 %collective-permute-start.9 = (f32[20,3,640]{2,1,0:T(4,128)S(1)}, f32[20,3,640]{2,1,0:T(4,128)S(1)}, u32[]{:S(2)}, u32[]{:S(2)}) collective-permute-start(f32[20,3,640]{2,1,0:T(4,128)S(1)} %pad_maximum_fusion.3), channel_id=1, source_target_pairs={{8,0},{16,8},{24,16},{9,1},{17,9},{25,17},{10,2},{18,10},{26,18},{... | collective-permute-start | bytes 460808 | tf_op jit(solution)/shard_map/ppermute | solution.py:186
  81.7 8.0 %collective-permute-start.8 = (f32[20,3,640]{2,1,0:T(4,128)S(1)}, f32[20,3,640]{2,1,0:T(4,128)S(1)}, u32[]{:S(2)}, u32[]{:S(2)}) collective-permute-start(f32[20,3,640]{2,1,0:T(4,128)S(1)} %pad_maximum_fusion.2), channel_id=1, source_target_pairs={{0,8},{8,16},{16,24},{1,9},{9,17},{17,25},{2,10},{10,18},{18,26},{... | collective-permute-start | bytes 460808 | tf_op jit(solution)/shard_map/ppermute | solution.py:186
  91.5 15.0 %collective-permute-start.10 = (f32[3,80,640]{2,1,0:T(8,128)S(1)}, f32[3,80,640]{2,1,0:T(8,128)S(1)}, u32[]{:S(2)}, u32[]{:S(2)}) collective-permute-start(f32[3,80,640]{2,1,0:T(8,128)S(1)} %get-tuple-element.50.refs_5_), channel_id=1, source_target_pairs={{0,1},{1,2},{2,3},{3,4},{4,5},{5,6},{6,7},{8,9},{9,10},{10,11},{11... | collective-permute-start | bytes 1843208 | tf_op jit(solution)/shard_map/ppermute | solution.py:186
  97.2 9.2 %collective-permute-start.11 = (f32[3,80,640]{2,1,0:T(8,128)S(1)}, f32[3,80,640]{2,1,0:T(8,128)S(1)}, u32[]{:S(2)}, u32[]{:S(2)}) collective-permute-start(f32[3,80,640]{2,1,0:T(8,128)S(1)} %get-tuple-element.51.refs_4_), channel_id=1, source_target_pairs={{1,0},{2,1},{3,2},{4,3},{5,4},{6,5},{7,6},{9,8},{10,9},{11,10},{12... | collective-permute-start | bytes 1843208 | tf_op jit(solution)/shard_map/ppermute | solution.py:186
  109.3 8.4 %collective-permute-start.12 = (f32[3]{0:T(128)S(1)}, f32[3]{0:T(128)S(1)}, u32[]{:S(2)}, u32[]{:S(2)}) collective-permute-start(f32[3]{0:T(128)S(1)} %maximum_reduce_fusion), channel_id=1, source_target_pairs={{0,1},{1,2},{2,3},{3,4},{4,5},{5,6},{6,7},{7,0},{8,9},{9,10},{10,1... | collective-permute-start | bytes 44 | tf_op jit(solution)/shard_map/ppermute | solution.py:193
  117.7 4.5 %collective-permute-start.13 = (f32[3]{0:T(128)S(1)}, f32[3]{0:T(128)S(1)}, u32[]{:S(2)}, u32[]{:S(2)}) collective-permute-start(f32[3]{0:T(128)S(1)} %max.27), channel_id=1, source_target_pairs={{0,2},{1,3},{2,4},{3,5},{4,6},{5,7},{6,0},{7,1},{8,10},{9,11},{10,... | collective-permute-start | bytes 44 | tf_op jit(solution)/shard_map/ppermute | solution.py:193
  122.2 3.6 %collective-permute-start.14 = (f32[3]{0:T(128)S(1)}, f32[3]{0:T(128)S(1)}, u32[]{:S(2)}, u32[]{:S(2)}) collective-permute-start(f32[3]{0:T(128)S(1)} %max.28), channel_id=1, source_target_pairs={{0,4},{1,5},{2,6},{3,7},{4,0},{5,1},{6,2},{7,3},{8,12},{9,13},{10,... | collective-permute-start | bytes 44 | tf_op jit(solution)/shard_map/ppermute | solution.py:193
  125.8 6.5 %collective-permute-start.15 = (f32[3]{0:T(128)S(1)}, f32[3]{0:T(128)S(1)}, u32[]{:S(2)}, u32[]{:S(2)}) collective-permute-start(f32[3]{0:T(128)S(1)} %max.29), channel_id=1, source_target_pairs={{0,8},{8,16},{16,24},{24,0},{1,9},{9,17},{17,25},{25,1},{2,10},{10... | collective-permute-start | bytes 44 | tf_op jit(solution)/shard_map/ppermute | solution.py:193
  132.3 4.5 %collective-permute-start.16 = (f32[3]{0:T(128)S(1)}, f32[3]{0:T(128)S(1)}, u32[]{:S(2)}, u32[]{:S(2)}) collective-permute-start(f32[3]{0:T(128)S(1)} %max.30), channel_id=1, source_target_pairs={{0,16},{8,24},{16,0},{24,8},{1,17},{9,25},{17,1},{25,9},{2,18},{10... | collective-permute-start | bytes 44 | tf_op jit(solution)/shard_map/ppermute | solution.py:193

commit v3 on v2

--- a/solution.py
+++ b/solution.py
@@ -13,16 +13,22 @@
 ROWS = 8
 
 
+def smear_cyclic(field, taps, axis):
+    length = field.shape[axis]
+
+    def ahead(value, count):
+        return pltpu.roll(value, (-count) % length, axis)
+
+    one = ahead(field, 1)
+    two = ahead(field, 2)
+    low = taps[0] * field + taps[1] * one + taps[2] * two
+    mid = taps[3] * field + taps[4] * one + taps[5] * two
+    return ahead(low, -RAD) + mid + ahead(taps[6] * field, RAD)
+
+
 def smear_x(row, taps):
-    length = row.shape[1]
     padded = jnp.concatenate([row, jnp.zeros((row.shape[0], LANES), row.dtype)], axis=1)
-    total = length + LANES
-    result = taps[RAD] * row
-    for k in range(2 * RAD + 1):
-        if k != RAD:
-            moved = pltpu.roll(padded, (RAD - k) % total, 1)
-            result = result + taps[k] * moved[:, :length]
-    return result
+    return smear_cyclic(padded, taps, 1)[:, : row.shape[1]]
 
 
 def smear_x_all(src, dst, taps):
@@ -43,19 +49,14 @@
 
 
 def smear_y(column, taps, height):
-    result = taps[RAD] * column[:height]
-    for k in range(2 * RAD + 1):
-        if k != RAD:
-            moved = pltpu.roll(column, (RAD - k) % (height + ROWS), 0)
-            result = result + taps[k] * moved[:height]
-    return result
+    return smear_cyclic(column, taps, 0)[:height]
 
 
 def taps_of(kernel_ref, row):
     return [kernel_ref[row, k] for k in range(2 * RAD + 1)]
 
 
-def rim_kernel(kernel_ref, u_ref, ylo_ref, yhi_ref, vtop_ref, vbot_ref, tail_ref):
+def rim_kernel(raw, kernel_ref, u_ref, ylo_ref, yhi_ref, vtop_ref, vbot_ref, tail_ref):
     planes = tail_ref.shape[0]
     have, height, length = u_ref.shape
     ky = taps_of(kernel_ref, 0)
@@ -64,6 +65,8 @@
         tail_ref[z] = jnp.zeros((ROWS, length), tail_ref.dtype)
         tail_ref[z, 0:RAD, :] = yhi_ref[z]
         tail_ref[z, ROWS - RAD : ROWS, :] = ylo_ref[z]
+        if raw:
+            tail_ref[z] = smear_x(tail_ref[z], taps_of(kernel_ref, 2))
         return 0
 
     lax.fori_loop(0, planes, fill, 0)
@@ -190,7 +193,11 @@
     count = lax.axis_size(axis)
     step = 1
     while step < count:
-        value = jnp.maximum(value, lax.ppermute(value, axis, [(i, (i + step) % count) for i in range(count)]))
+        if count & (count - 1) == 0:
+            pairs = [(i, i ^ step) for i in range(count)]
+        else:
+            pairs = [(i, (i + step) % count) for i in range(count)]
+        value = jnp.maximum(value, lax.ppermute(value, axis, pairs))
         step *= 2
     return value
 
@@ -237,14 +244,14 @@
     for iteration in range(ITERS):
         last = iteration == ITERS - 1
         if iteration == 0:
-            yend, yfirst = u[:, height - RAD :], u[:, :RAD]
+            yend, yfirst = d[:, height - RAD :], d[:, :RAD]
         else:
             parts = (u_rims[:RAD], u[RAD : planes - RAD], u_rims[RAD:])
             yend = jnp.concatenate([part[:, height - RAD :] for part in parts], axis=0)
             yfirst = jnp.concatenate([part[:, :RAD] for part in parts], axis=0)
         ylo = from_neighbour(yend, "gy", -1)
         yhi = from_neighbour(yfirst, "gy", 1)
-        vtop, vbot, tail = call(rim_kernel, [rim, rim, tails], [u_rims, ylo, yhi], name="rim")
+        vtop, vbot, tail = call(functools.partial(rim_kernel, iteration == 0), [rim, rim, tails], [u_rims, ylo, yhi], name="rim")
         zlo = from_neighbour(vbot, "gz", -1)
         zhi = from_neighbour(vtop, "gz", 1)
         state = [whole] if last else [whole, whole]

time: 138 us -> 135 us (0.978)
  waiting for transfers between devices: 26.7 us -> 17.5 us
  Pallas kernels: 55.5 us -> 61.2 us
    ppermute x12, waiting for transfers between devices: 13.6 us -> 6.51 us  [from_neighbour(): return lax.ppermute(block, axis, pairs)]
    pallas_call x10, Pallas kernels: 55.5 us -> 61.2 us  [call(): pl.pallas_call(body, out_shape=outs, in_specs=in_specs, out_specs=out_spe...]
    ppermute x5, waiting for transfers between devices: 13 us -> 11 us  [max_over(): value = jnp.maximum(value, lax.ppermute(value, axis, pairs))]
  transfers between devices with their start and end apart: 17 -> 17, of which waited for: 11 -> 9; matrix products, arithmetic and copies ran while one was open for 0% -> 1% of each run, Pallas kernels for 22% -> 30%
where the time goes in v3:
time: 135 us
  Pallas kernels  61.2 us (45%)
  starting transfers between devices  49.4 us (37%)
  waiting for transfers between devices  17.5 us (13%)
  local copies, waits for them, and re-layouts  3.53 us (3%)
  other arithmetic  2.38 us (2%)
    pallas_call x10, Pallas kernels, call(): pl.pallas_call(body, out_shape=outs, in_specs=in_specs, out_specs=out_spe...  61.2 us
    ppermute x12, starting transfers between devices, from_neighbour(): return lax.ppermute(block, axis, pairs)  34.9 us
    ppermute x5, starting transfers between devices, max_over(): value = jnp.maximum(value, lax.ppermute(value, axis, pairs))  14.5 us
    ppermute x5, waiting for transfers between devices, max_over(): value = jnp.maximum(value, lax.ppermute(value, axis, pairs))  11 us
    ppermute x12, waiting for transfers between devices, from_neighbour(): return lax.ppermute(block, axis, pairs)  6.51 us
  transfers between devices with their start and end apart: 17, of which 9 were waited for; matrix products, arithmetic and copies ran while one was open for 1% of the time, Pallas kernels for 30%

profile of v3, /device:TPU:0, one launch (start us, length us, event | category | flops | bytes accessed | tf_op | source)
XLA Modules:
  0.0 135.0 jit_solution(13445006040927945393)
XLA Ops:
  0.6 1.2 fusion.2
  1.8 5.0 %collective-permute-start = (f32[20,3,640]{2,1,0:T(4,128)S(1)}, f32[20,3,640]{2,1,0:T(4,128)S(1)}, u32[]{:S(2)}, u32[]{:S(2)}) collective-permute-start(f32[20,3,640]{2,1,0:T(4,128)S(1)} %get-tuple-element.69), channel_id=1, source_target_pairs={{0,8},{8,16},{16,24},{1,9},{9,17},{17,25},{2,10},{10,18},{18,26},{... | collective-permute-start | bytes 460808 | tf_op jit(solution)/shard_map/ppermute | solution.py:189
  6.8 1.3 collective-permute-start.1
  8.1 0.8 reduce_sum.9
  8.9 0.8 broadcast_divide_fusion.kernel_ref.refs_0_
  9.7 0.0 copy-start
  9.7 2.2 %copy-done = f32[80,20,640]{2,0,1:T(8,128)S(1)} copy-done((f32[80,20,640]{2,0,1:T(8,128)S(1)}, f32[80,20,640]{2,0,1:T(8,128)}, u32[]{:S(2)}) %copy-start) | copy-done | bytes 4096024
  11.8 9.7 %first.1.u_ref.refs_2_ = f32[20,80,640]{2,1,0:T(8,128)S(1)} custom-call(f32[3,7]{1,0:T(4,128)S(1)} %broadcast_divide_fusion.kernel_ref.refs_0_, f32[20,80,640]{2,1,0:T(8,128)S(1)} %bitcast.9), custom_call_target="tpu_custom_call" | custom-call | tf_op jit(solution)/shard_map/first/pallas_call | solution.py:227
  21.5 0.0 copy-start.1
  21.6 0.0 collective-permute-done.ylo_ref
  21.6 0.0 collective-permute-done.1.yhi_ref
  21.6 4.9 %rim.3 = (f32[3,80,640]{2,1,0:T(8,128)S(1)}, f32[3,80,640]{2,1,0:T(8,128)S(1)}, f32[20,8,640]{2,1,0:T(8,128)S(1)}) custom-call(f32[3,7]{1,0:T(4,128)S(1)} %broadcast_divide_fusion.kernel_ref.refs_0_, f32[20,80,640]{2,1,0:T(8,128)S(1)} %first.1.u_ref.refs_2_, f32[20,3,640]{2,1,0:T(4,128)S(1)} %collective-permute-done.ylo_ref, ...), custom_call_target="tpu_custom_call" | custom-call | tf_op jit(solution)/shard_map/rim/pallas_call | solution.py:227
  26.5 1.5 %collective-permute-start.2 = (f32[3,80,640]{2,1,0:T(8,128)S(1)}, f32[3,80,640]{2,1,0:T(8,128)S(1)}, u32[]{:S(2)}, u32[]{:S(2)}) collective-permute-start(f32[3,80,640]{2,1,0:T(8,128)S(1)} %get-tuple-element.33.refs_5_), channel_id=1, source_target_pairs={{0,1},{1,2},{2,3},{3,4},{4,5},{5,6},{6,7},{8,9},{9,10},{10,11},{11... | collective-permute-start | bytes 1843208 | tf_op jit(solution)/shard_map/ppermute | solution.py:189
  28.0 1.3 collective-permute-start.3
  29.3 0.0 copy-done.1
  29.3 11.9 %inner.3 = (f32[20,80,640]{2,1,0:T(8,128)S(1)}, f32[20,80,640]{2,1,0:T(8,128)S(1)}, f32[8,128]{1,0:T(8,128)S(1)}, f32[3,80,640]{2,1,0:T(8,128)S(1)}, f32[3,80,640]{2,1,0:T(8,128)S(1)}) custom-call(f32[3,7]{1,0:T(4,128)S(1)} %broadcast_divide_fusion.kernel_ref.refs_0_, f32[20,80,640]{2,1,0:T(8,128)S(1)} %bitcast.10, f32[20,80,640]{2,1,0:T(8,128)S(1)} %first.1.u_ref.refs_2_, ...), custom_call_target="tpu_custom_call" | custom-call | tf_op jit(solution)/shard_map/inner/pallas_call | solution.py:227
  41.2 0.1 fusion.1
  41.3 0.0 collective-permute-done.2.refs_2_
  41.3 0.0 collective-permute-done.3.refs_3_
  41.3 4.5 %edge.3 = (f32[6,80,640]{2,1,0:T(8,128)S(1)}, f32[6,80,640]{2,1,0:T(8,128)S(1)}, f32[8,128]{1,0:T(8,128)S(1)}) custom-call(f32[3,7]{1,0:T(4,128)S(1)} %broadcast_divide_fusion.kernel_ref.refs_0_, f32[20,80,640]{2,1,0:T(8,128)S(1)} %bitcast.11, f32[3,80,640]{2,1,0:T(8,128)S(1)} %collective-permute-done.2.refs_2_, ...), custom_call_target="tpu_custom_call" | custom-call | tf_op jit(solution)/shard_map/edge/pallas_call | solution.py:227
  45.9 1.3 collective-permute-start.5
  47.3 5.0 %collective-permute-start.4 = (f32[20,3,640]{2,1,0:T(4,128)S(1)}, f32[20,3,640]{2,1,0:T(4,128)S(1)}, u32[]{:S(2)}, u32[]{:S(2)}) collective-permute-start(f32[20,3,640]{2,1,0:T(4,128)S(1)} %pad_maximum_fusion), channel_id=1, source_target_pairs={{0,8},{8,16},{16,24},{1,9},{9,17},{17,25},{2,10},{10,18},{18,26},{... | collective-permute-start | bytes 460808 | tf_op jit(solution)/shard_map/ppermute | solution.py:189
  52.3 1.7 %collective-permute-done.5.yhi_ref = f32[20,3,640]{2,1,0:T(4,128)S(1)} collective-permute-done((f32[20,3,640]{2,1,0:T(4,128)S(1)}, f32[20,3,640]{2,1,0:T(4,128)S(1)}, u32[]{:S(2)}, u32[]{:S(2)}) %collective-permute-start.5) | collective-permute-done | bytes 153632 | tf_op jit(solution)/shard_map/ppermute | solution.py:189
  54.0 1.5 %collective-permute-done.4.ylo_ref = f32[20,3,640]{2,1,0:T(4,128)S(1)} collective-permute-done((f32[20,3,640]{2,1,0:T(4,128)S(1)}, f32[20,3,640]{2,1,0:T(4,128)S(1)}, u32[]{:S(2)}, u32[]{:S(2)}) %collective-permute-start.4) | collective-permute-done | bytes 153632 | tf_op jit(solution)/shard_map/ppermute | solution.py:189
  55.5 1.7 %rim.4 = (f32[3,80,640]{2,1,0:T(8,128)S(1)}, f32[3,80,640]{2,1,0:T(8,128)S(1)}, f32[20,8,640]{2,1,0:T(8,128)S(1)}) custom-call(f32[3,7]{1,0:T(4,128)S(1)} %broadcast_divide_fusion.kernel_ref.refs_0_, f32[6,80,640]{2,1,0:T(8,128)S(1)} %get-tuple-element.39.u_ref, f32[20,3,640]{2,1,0:T(4,128)S(1)} %collective-permute-done.4.ylo_ref, ...), custom_call_target="tpu_custom_call" | custom-call | tf_op jit(solution)/shard_map/rim/pallas_call | solution.py:227
  57.2 5.3 %collective-permute-start.6 = (f32[3,80,640]{2,1,0:T(8,128)S(1)}, f32[3,80,640]{2,1,0:T(8,128)S(1)}, u32[]{:S(2)}, u32[]{:S(2)}) collective-permute-start(f32[3,80,640]{2,1,0:T(8,128)S(1)} %get-tuple-element.41.refs_5_), channel_id=1, source_target_pairs={{0,1},{1,2},{2,3},{3,4},{4,5},{5,6},{6,7},{8,9},{9,10},{10,11},{11... | collective-permute-start | bytes 1843208 | tf_op jit(solution)/shard_map/ppermute | solution.py:189
  62.5 1.3 collective-permute-start.7
  63.8 11.9 %inner.4 = (f32[20,80,640]{2,1,0:T(8,128)S(1)}, f32[20,80,640]{2,1,0:T(8,128)S(1)}, f32[8,128]{1,0:T(8,128)S(1)}, f32[3,80,640]{2,1,0:T(8,128)S(1)}, f32[3,80,640]{2,1,0:T(8,128)S(1)}) custom-call(f32[3,7]{1,0:T(4,128)S(1)} %broadcast_divide_fusion.kernel_ref.refs_0_, f32[20,80,640]{2,1,0:T(8,128)S(1)} %get-tuple-element.43.refs_1_, ...), custom_call_target="tpu_custom_call" | custom-call | tf_op jit(solution)/shard_map/inner/pallas_call | solution.py:227
  75.7 0.1 fusion
  75.8 0.0 collective-permute-done.6.refs_2_
  75.8 0.0 collective-permute-done.7.refs_3_
  75.8 4.6 %edge.4 = (f32[6,80,640]{2,1,0:T(8,128)S(1)}, f32[6,80,640]{2,1,0:T(8,128)S(1)}, f32[8,128]{1,0:T(8,128)S(1)}) custom-call(f32[3,7]{1,0:T(4,128)S(1)} %broadcast_divide_fusion.kernel_ref.refs_0_, f32[6,80,640]{2,1,0:T(8,128)S(1)} %get-tuple-element.38.refs_1_, f32[3,80,640]{2,1,0:T(8,128)S(1)} %collective-permute-done.6.refs_2_, ...), custom_call_target="tpu_custom_call" | custom-call | tf_op jit(solution)/shard_map/edge/pallas_call | solution.py:227
  80.5 1.3 collective-permute-start.9
  81.8 4.7 %collective-permute-start.8 = (f32[20,3,640]{2,1,0:T(4,128)S(1)}, f32[20,3,640]{2,1,0:T(4,128)S(1)}, u32[]{:S(2)}, u32[]{:S(2)}) collective-permute-start(f32[20,3,640]{2,1,0:T(4,128)S(1)} %pad_maximum_fusion.2), channel_id=1, source_target_pairs={{0,8},{8,16},{16,24},{1,9},{9,17},{17,25},{2,10},{10,18},{18,26},{... | collective-permute-start | bytes 460808 | tf_op jit(solution)/shard_map/ppermute | solution.py:189
  86.6 1.7 %collective-permute-done.9.yhi_ref = f32[20,3,640]{2,1,0:T(4,128)S(1)} collective-permute-done((f32[20,3,640]{2,1,0:T(4,128)S(1)}, f32[20,3,640]{2,1,0:T(4,128)S(1)}, u32[]{:S(2)}, u32[]{:S(2)}) %collective-permute-start.9) | collective-permute-done | bytes 153632 | tf_op jit(solution)/shard_map/ppermute | solution.py:189
  88.3 1.5 %collective-permute-done.8.ylo_ref = f32[20,3,640]{2,1,0:T(4,128)S(1)} collective-permute-done((f32[20,3,640]{2,1,0:T(4,128)S(1)}, f32[20,3,640]{2,1,0:T(4,128)S(1)}, u32[]{:S(2)}, u32[]{:S(2)}) %collective-permute-start.8) | collective-permute-done | bytes 153632 | tf_op jit(solution)/shard_map/ppermute | solution.py:189
  89.8 1.7 %rim.5 = (f32[3,80,640]{2,1,0:T(8,128)S(1)}, f32[3,80,640]{2,1,0:T(8,128)S(1)}, f32[20,8,640]{2,1,0:T(8,128)S(1)}) custom-call(f32[3,7]{1,0:T(4,128)S(1)} %broadcast_divide_fusion.kernel_ref.refs_0_, f32[6,80,640]{2,1,0:T(8,128)S(1)} %get-tuple-element.48.u_ref, f32[20,3,640]{2,1,0:T(4,128)S(1)} %collective-permute-done.8.ylo_ref, ...), custom_call_target="tpu_custom_call" | custom-call | tf_op jit(solution)/shard_map/rim/pallas_call | solution.py:227
  91.5 5.7 %collective-permute-start.10 = (f32[3,80,640]{2,1,0:T(8,128)S(1)}, f32[3,80,640]{2,1,0:T(8,128)S(1)}, u32[]{:S(2)}, u32[]{:S(2)}) collective-permute-start(f32[3,80,640]{2,1,0:T(8,128)S(1)} %get-tuple-element.50.refs_5_), channel_id=1, source_target_pairs={{0,1},{1,2},{2,3},{3,4},{4,5},{5,6},{6,7},{8,9},{9,10},{10,11},{11... | collective-permute-start | bytes 1843208 | tf_op jit(solution)/shard_map/ppermute | solution.py:189
  97.2 1.3 collective-permute-start.11
  98.5 7.6 %inner.5 = (f32[20,80,640]{2,1,0:T(8,128)}, f32[8,128]{1,0:T(8,128)S(1)}, f32[3,80,640]{2,1,0:T(8,128)S(1)}, f32[3,80,640]{2,1,0:T(8,128)S(1)}) custom-call(f32[3,7]{1,0:T(4,128)S(1)} %broadcast_divide_fusion.kernel_ref.refs_0_, f32[20,80,640]{2,1,0:T(8,128)S(1)} %get-tuple-element.52.refs_1_, f32[20,80,640]{2,1,0:T(8,128)S(1)} %get-tuple-element.49.refs_2_, ...), custom_call_target="tpu_custom_call" | custom-call | tf_op jit(solution)/shard_map/inner/pallas_call | solution.py:227
  106.1 0.0 collective-permute-done.10.refs_2_
  106.1 0.0 collective-permute-done.11.refs_3_
  106.1 2.7 %edge.5 = (f32[20,80,640]{2,1,0:T(8,128)}, f32[8,128]{1,0:T(8,128)S(1)}) custom-call(f32[3,7]{1,0:T(4,128)S(1)} %broadcast_divide_fusion.kernel_ref.refs_0_, f32[6,80,640]{2,1,0:T(8,128)S(1)} %get-tuple-element.47.refs_1_, f32[3,80,640]{2,1,0:T(8,128)S(1)} %collective-permute-done.10.refs_2_, ...), custom_call_target="tpu_custom_call", output_to_operand_aliasing={{0}: (9, {})} | custom-call | tf_op jit(solution)/shard_map/edge/pallas_call | solution.py:227
  108.8 0.1 maximum_reduce_fusion
  108.9 8.5 %collective-permute-start.12 = (f32[3]{0:T(128)S(1)}, f32[3]{0:T(128)S(1)}, u32[]{:S(2)}, u32[]{:S(2)}) collective-permute-start(f32[3]{0:T(128)S(1)} %maximum_reduce_fusion), channel_id=1, source_target_pairs={{0,1},{1,0},{2,3},{3,2},{4,5},{5,4},{6,7},{7,6},{8,9},{9,8},{10,11... | collective-permute-start | bytes 44 | tf_op jit(solution)/shard_map/ppermute | solution.py:200
  117.4 0.8 collective-permute-done.12
  118.3 0.1 collective-permute-start.13
  118.3 3.5 %collective-permute-done.13 = f32[3]{0:T(128)S(1)} collective-permute-done((f32[3]{0:T(128)S(1)}, f32[3]{0:T(128)S(1)}, u32[]{:S(2)}, u32[]{:S(2)}) %collective-permute-start.13) | collective-permute-done | bytes 44 | tf_op jit(solution)/shard_map/ppermute | solution.py:200
  121.8 0.0 collective-permute-start.14
  121.8 3.6 %collective-permute-done.14 = f32[3]{0:T(128)S(1)} collective-permute-done((f32[3]{0:T(128)S(1)}, f32[3]{0:T(128)S(1)}, u32[]{:S(2)}, u32[]{:S(2)}) %collective-permute-start.14) | collective-permute-done | bytes 44 | tf_op jit(solution)/shard_map/ppermute | solution.py:200
  125.4 2.5 %collective-permute-start.15 = (f32[3]{0:T(128)S(1)}, f32[3]{0:T(128)S(1)}, u32[]{:S(2)}, u32[]{:S(2)}) collective-permute-start(f32[3]{0:T(128)S(1)} %max.29), channel_id=1, source_target_pairs={{0,8},{8,0},{16,24},{24,16},{1,9},{9,1},{17,25},{25,17},{2,10},{10... | collective-permute-start | bytes 44 | tf_op jit(solution)/shard_map/ppermute | solution.py:200
  127.9 1.5 %collective-permute-done.15 = f32[3]{0:T(128)S(1)} collective-permute-done((f32[3]{0:T(128)S(1)}, f32[3]{0:T(128)S(1)}, u32[]{:S(2)}, u32[]{:S(2)}) %collective-permute-start.15) | collective-permute-done | bytes 44 | tf_op jit(solution)/shard_map/ppermute | solution.py:200
  129.4 3.5 %collective-permute-start.16 = (f32[3]{0:T(128)S(1)}, f32[3]{0:T(128)S(1)}, u32[]{:S(2)}, u32[]{:S(2)}) collective-permute-start(f32[3]{0:T(128)S(1)} %max.30), channel_id=1, source_target_pairs={{0,16},{8,24},{16,0},{24,8},{1,17},{9,25},{17,1},{25,9},{2,18},{10... | collective-permute-start | bytes 44 | tf_op jit(solution)/shard_map/ppermute | solution.py:200
  132.9 1.5 %collective-permute-done.16 = f32[3]{0:T(128)S(1)} collective-permute-done((f32[3]{0:T(128)S(1)}, f32[3]{0:T(128)S(1)}, u32[]{:S(2)}, u32[]{:S(2)}) %collective-permute-start.16) | collective-permute-done | bytes 44 | tf_op jit(solution)/shard_map/ppermute | solution.py:200
  134.5 0.5 max.31
  (12 shorter events, 0.3 us)
Async XLA Ops:
  1.8 19.7 %collective-permute-start = (f32[20,3,640]{2,1,0:T(4,128)S(1)}, f32[20,3,640]{2,1,0:T(4,128)S(1)}, u32[]{:S(2)}, u32[]{:S(2)}) collective-permute-start(f32[20,3,640]{2,1,0:T(4,128)S(1)} %get-tuple-element.69), channel_id=1, source_target_pairs={{0,8},{8,16},{16,24},{1,9},{9,17},{17,25},{2,10},{10,18},{18,26},{... | collective-permute-start | bytes 460808 | tf_op jit(solution)/shard_map/ppermute | solution.py:189
  6.8 14.8 %collective-permute-start.1 = (f32[20,3,640]{2,1,0:T(4,128)S(1)}, f32[20,3,640]{2,1,0:T(4,128)S(1)}, u32[]{:S(2)}, u32[]{:S(2)}) collective-permute-start(f32[20,3,640]{2,1,0:T(4,128)S(1)} %get-tuple-element.68), channel_id=1, source_target_pairs={{8,0},{16,8},{24,16},{9,1},{17,9},{25,17},{10,2},{18,10},{26,18},{... | collective-permute-start | bytes 460808 | tf_op jit(solution)/shard_map/ppermute | solution.py:189
  9.7 2.2 %copy-start = (f32[80,20,640]{2,0,1:T(8,128)S(1)}, f32[80,20,640]{2,0,1:T(8,128)}, u32[]{:S(2)}) copy-start(f32[80,20,640]{2,0,1:T(8,128)} %param.2) | copy-start | bytes 12288004
  21.5 7.7 %copy-start.1 = (f32[80,20,640]{2,0,1:T(8,128)S(1)}, f32[80,20,640]{2,0,1:T(8,128)}, u32[]{:S(2)}) copy-start(f32[80,20,640]{2,0,1:T(8,128)} %param.2) | copy-start | bytes 12288004
  26.5 14.8 %collective-permute-start.2 = (f32[3,80,640]{2,1,0:T(8,128)S(1)}, f32[3,80,640]{2,1,0:T(8,128)S(1)}, u32[]{:S(2)}, u32[]{:S(2)}) collective-permute-start(f32[3,80,640]{2,1,0:T(8,128)S(1)} %get-tuple-element.33.refs_5_), channel_id=1, source_target_pairs={{0,1},{1,2},{2,3},{3,4},{4,5},{5,6},{6,7},{8,9},{9,10},{10,11},{11... | collective-permute-start | bytes 1843208 | tf_op jit(solution)/shard_map/ppermute | solution.py:189
  28.0 13.3 %collective-permute-start.3 = (f32[3,80,640]{2,1,0:T(8,128)S(1)}, f32[3,80,640]{2,1,0:T(8,128)S(1)}, u32[]{:S(2)}, u32[]{:S(2)}) collective-permute-start(f32[3,80,640]{2,1,0:T(8,128)S(1)} %get-tuple-element.34.refs_4_), channel_id=1, source_target_pairs={{1,0},{2,1},{3,2},{4,3},{5,4},{6,5},{7,6},{9,8},{10,9},{11,10},{12... | collective-permute-start | bytes 1843208 | tf_op jit(solution)/shard_map/ppermute | solution.py:189
  45.9 8.1 %collective-permute-start.5 = (f32[20,3,640]{2,1,0:T(4,128)S(1)}, f32[20,3,640]{2,1,0:T(4,128)S(1)}, u32[]{:S(2)}, u32[]{:S(2)}) collective-permute-start(f32[20,3,640]{2,1,0:T(4,128)S(1)} %pad_maximum_fusion.1), channel_id=1, source_target_pairs={{8,0},{16,8},{24,16},{9,1},{17,9},{25,17},{10,2},{18,10},{26,18},{... | collective-permute-start | bytes 460808 | tf_op jit(solution)/shard_map/ppermute | solution.py:189
  47.3 8.3 %collective-permute-start.4 = (f32[20,3,640]{2,1,0:T(4,128)S(1)}, f32[20,3,640]{2,1,0:T(4,128)S(1)}, u32[]{:S(2)}, u32[]{:S(2)}) collective-permute-start(f32[20,3,640]{2,1,0:T(4,128)S(1)} %pad_maximum_fusion), channel_id=1, source_target_pairs={{0,8},{8,16},{16,24},{1,9},{9,17},{17,25},{2,10},{10,18},{18,26},{... | collective-permute-start | bytes 460808 | tf_op jit(solution)/shard_map/ppermute | solution.py:189
  57.2 18.6 %collective-permute-start.6 = (f32[3,80,640]{2,1,0:T(8,128)S(1)}, f32[3,80,640]{2,1,0:T(8,128)S(1)}, u32[]{:S(2)}, u32[]{:S(2)}) collective-permute-start(f32[3,80,640]{2,1,0:T(8,128)S(1)} %get-tuple-element.41.refs_5_), channel_id=1, source_target_pairs={{0,1},{1,2},{2,3},{3,4},{4,5},{5,6},{6,7},{8,9},{9,10},{10,11},{11... | collective-permute-start | bytes 1843208 | tf_op jit(solution)/shard_map/ppermute | solution.py:189
  62.5 13.3 %collective-permute-start.7 = (f32[3,80,640]{2,1,0:T(8,128)S(1)}, f32[3,80,640]{2,1,0:T(8,128)S(1)}, u32[]{:S(2)}, u32[]{:S(2)}) collective-permute-start(f32[3,80,640]{2,1,0:T(8,128)S(1)} %get-tuple-element.42.refs_4_), channel_id=1, source_target_pairs={{1,0},{2,1},{3,2},{4,3},{5,4},{6,5},{7,6},{9,8},{10,9},{11,10},{12... | collective-permute-start | bytes 1843208 | tf_op jit(solution)/shard_map/ppermute | solution.py:189
  80.5 7.8 %collective-permute-start.9 = (f32[20,3,640]{2,1,0:T(4,128)S(1)}, f32[20,3,640]{2,1,0:T(4,128)S(1)}, u32[]{:S(2)}, u32[]{:S(2)}) collective-permute-start(f32[20,3,640]{2,1,0:T(4,128)S(1)} %pad_maximum_fusion.3), channel_id=1, source_target_pairs={{8,0},{16,8},{24,16},{9,1},{17,9},{25,17},{10,2},{18,10},{26,18},{... | collective-permute-start | bytes 460808 | tf_op jit(solution)/shard_map/ppermute | solution.py:189
  81.8 8.0 %collective-permute-start.8 = (f32[20,3,640]{2,1,0:T(4,128)S(1)}, f32[20,3,640]{2,1,0:T(4,128)S(1)}, u32[]{:S(2)}, u32[]{:S(2)}) collective-permute-start(f32[20,3,640]{2,1,0:T(4,128)S(1)} %pad_maximum_fusion.2), channel_id=1, source_target_pairs={{0,8},{8,16},{16,24},{1,9},{9,17},{17,25},{2,10},{10,18},{18,26},{... | collective-permute-start | bytes 460808 | tf_op jit(solution)/shard_map/ppermute | solution.py:189
  91.5 14.6 %collective-permute-start.10 = (f32[3,80,640]{2,1,0:T(8,128)S(1)}, f32[3,80,640]{2,1,0:T(8,128)S(1)}, u32[]{:S(2)}, u32[]{:S(2)}) collective-permute-start(f32[3,80,640]{2,1,0:T(8,128)S(1)} %get-tuple-element.50.refs_5_), channel_id=1, source_target_pairs={{0,1},{1,2},{2,3},{3,4},{4,5},{5,6},{6,7},{8,9},{9,10},{10,11},{11... | collective-permute-start | bytes 1843208 | tf_op jit(solution)/shard_map/ppermute | solution.py:189
  97.2 8.9 %collective-permute-start.11 = (f32[3,80,640]{2,1,0:T(8,128)S(1)}, f32[3,80,640]{2,1,0:T(8,128)S(1)}, u32[]{:S(2)}, u32[]{:S(2)}) collective-permute-start(f32[3,80,640]{2,1,0:T(8,128)S(1)} %get-tuple-element.51.refs_4_), channel_id=1, source_target_pairs={{1,0},{2,1},{3,2},{4,3},{5,4},{6,5},{7,6},{9,8},{10,9},{11,10},{12... | collective-permute-start | bytes 1843208 | tf_op jit(solution)/shard_map/ppermute | solution.py:189
  108.9 9.3 %collective-permute-start.12 = (f32[3]{0:T(128)S(1)}, f32[3]{0:T(128)S(1)}, u32[]{:S(2)}, u32[]{:S(2)}) collective-permute-start(f32[3]{0:T(128)S(1)} %maximum_reduce_fusion), channel_id=1, source_target_pairs={{0,1},{1,0},{2,3},{3,2},{4,5},{5,4},{6,7},{7,6},{8,9},{9,8},{10,11... | collective-permute-start | bytes 44 | tf_op jit(solution)/shard_map/ppermute | solution.py:200
  118.3 3.6 %collective-permute-start.13 = (f32[3]{0:T(128)S(1)}, f32[3]{0:T(128)S(1)}, u32[]{:S(2)}, u32[]{:S(2)}) collective-permute-start(f32[3]{0:T(128)S(1)} %max.27), channel_id=1, source_target_pairs={{0,2},{1,3},{2,0},{3,1},{4,6},{5,7},{6,4},{7,5},{8,10},{9,11},{10,... | collective-permute-start | bytes 44 | tf_op jit(solution)/shard_map/ppermute | solution.py:200
  121.8 3.6 %collective-permute-start.14 = (f32[3]{0:T(128)S(1)}, f32[3]{0:T(128)S(1)}, u32[]{:S(2)}, u32[]{:S(2)}) collective-permute-start(f32[3]{0:T(128)S(1)} %max.28), channel_id=1, source_target_pairs={{0,4},{1,5},{2,6},{3,7},{4,0},{5,1},{6,2},{7,3},{8,12},{9,13},{10,... | collective-permute-start | bytes 44 | tf_op jit(solution)/shard_map/ppermute | solution.py:200
  125.4 4.0 %collective-permute-start.15 = (f32[3]{0:T(128)S(1)}, f32[3]{0:T(128)S(1)}, u32[]{:S(2)}, u32[]{:S(2)}) collective-permute-start(f32[3]{0:T(128)S(1)} %max.29), channel_id=1, source_target_pairs={{0,8},{8,0},{16,24},{24,16},{1,9},{9,1},{17,25},{25,17},{2,10},{10... | collective-permute-start | bytes 44 | tf_op jit(solution)/shard_map/ppermute | solution.py:200
  129.4 5.0 %collective-permute-start.16 = (f32[3]{0:T(128)S(1)}, f32[3]{0:T(128)S(1)}, u32[]{:S(2)}, u32[]{:S(2)}) collective-permute-start(f32[3]{0:T(128)S(1)} %max.30), channel_id=1, source_target_pairs={{0,16},{8,24},{16,0},{24,8},{1,17},{9,25},{17,1},{25,9},{2,18},{10... | collective-permute-start | bytes 44 | tf_op jit(solution)/shard_map/ppermute | solution.py:200

commit v4 on v3

--- a/solution.py
+++ b/solution.py
@@ -26,26 +26,51 @@
     return ahead(low, -RAD) + mid + ahead(taps[6] * field, RAD)
 
 
-def smear_x(row, taps):
-    padded = jnp.concatenate([row, jnp.zeros((row.shape[0], LANES), row.dtype)], axis=1)
-    return smear_cyclic(padded, taps, 1)[:, : row.shape[1]]
-
-
-def smear_x_all(src, dst, taps):
-    planes, height, _ = src.shape
-    chunk = 2 * ROWS if height % (2 * ROWS) == 0 else ROWS
-
-    def body(z, _):
-        for y in range(0, height, chunk):
-            dst[z, y : y + chunk, :] = smear_x(src[z, y : y + chunk, :], taps)
+def band_of(taps, length):
+    row = lax.broadcasted_iota(jnp.int32, (length, length), 0)
+    col = lax.broadcasted_iota(jnp.int32, (length, length), 1)
+    band = jnp.zeros((length, length), taps.dtype)
+    for k in range(2 * RAD + 1):
+        band = jnp.where(row - col == k - RAD, taps[k], band)
+    high = lax.reduce_precision(band, 8, 7)
+    return jnp.stack([high.astype(jnp.bfloat16), (band - high).astype(jnp.bfloat16)])
+
+
+def smear_x(rows, band_ref, store):
+    length = rows.shape[1]
+    high = rows.astype(jnp.bfloat16)
+    low = (rows - high.astype(jnp.float32)).astype(jnp.bfloat16)
+    for begin in range(0, length, 2 * LANES):
+        end = min(begin + 2 * LANES, length)
+        first = max(begin - LANES, 0)
+        stop = min(end + LANES, length)
+
+        def product(a, n):
+            return jnp.dot(
+                a[:, first:stop], band_ref[n, first:stop, begin:end], preferred_element_type=jnp.float32
+            )
+
+        store(slice(begin, end), product(high, 0) + product(low, 0) + product(high, 1))
+
+
+def smear_planes(src, dst, band_ref, begin, count):
+    _, height, length = src.shape
+    group = max(n for n in range(1, 8) if count % n == 0)
+
+    def body(i, _):
+        at = pl.ds(begin + i * group, group)
+
+        def store(cols, value):
+            dst[at, :, cols] = value.reshape(group, height, value.shape[1])
+
+        smear_x(src[at].reshape(group * height, length), band_ref, store)
         return 0
 
-    lax.fori_loop(0, planes, body, 0)
-
-
-def first_kernel(kernel_ref, d_ref, u_ref):
-    taps = [kernel_ref[2, k] for k in range(2 * RAD + 1)]
-    smear_x_all(d_ref, u_ref, taps)
+    lax.fori_loop(0, count // group, body, 0)
+
+
+def first_kernel(kernel_ref, d_ref, band_ref, u_ref):
+    smear_planes(d_ref, u_ref, band_ref, 0, d_ref.shape[0])
 
 
 def smear_y(column, taps, height):
@@ -56,7 +81,8 @@
     return [kernel_ref[row, k] for k in range(2 * RAD + 1)]
 
 
-def rim_kernel(raw, kernel_ref, u_ref, ylo_ref, yhi_ref, vtop_ref, vbot_ref, tail_ref):
+def rim_kernel(raw, kernel_ref, u_ref, ylo_ref, yhi_ref, *refs):
+    vtop_ref, vbot_ref, tail_ref = refs[-3:]
     planes = tail_ref.shape[0]
     have, height, length = u_ref.shape
     ky = taps_of(kernel_ref, 0)
@@ -65,11 +91,11 @@
         tail_ref[z] = jnp.zeros((ROWS, length), tail_ref.dtype)
         tail_ref[z, 0:RAD, :] = yhi_ref[z]
         tail_ref[z, ROWS - RAD : ROWS, :] = ylo_ref[z]
-        if raw:
-            tail_ref[z] = smear_x(tail_ref[z], taps_of(kernel_ref, 2))
         return 0
 
     lax.fori_loop(0, planes, fill, 0)
+    if raw:
+        smear_planes(tail_ref, tail_ref, refs[0], 0, planes)
     for x in range(0, length, LANES):
         cols = slice(x, x + LANES)
 
@@ -96,23 +122,11 @@
     dev_ref[...] = jnp.maximum(dev_ref[...], off)
 
 
-def smear_planes(src, dst, taps, begin, count):
-    height = src.shape[1]
-    chunk = 2 * ROWS if height % (2 * ROWS) == 0 else ROWS
-
-    def body(z, _):
-        for y in range(0, height, chunk):
-            dst[z, y : y + chunk, :] = smear_x(src[z, y : y + chunk, :], taps)
-        return 0
-
-    lax.fori_loop(begin, begin + count, body, 0)
-
-
 def inner_kernel(last, *refs):
     if last:
         kernel_ref, p_ref, u_ref, tail_ref, vtop_ref, vbot_ref, d_ref, out_ref, dev_ref, below_ref, above_ref, v = refs
     else:
-        kernel_ref, p_ref, u_ref, tail_ref, vtop_ref, vbot_ref, out_ref, unext_ref, dev_ref, below_ref, above_ref, v = refs
+        kernel_ref, p_ref, u_ref, tail_ref, vtop_ref, vbot_ref, band_ref, out_ref, unext_ref, dev_ref, below_ref, above_ref, v = refs
         d_ref = None
     planes, height, length = p_ref.shape
     ky = taps_of(kernel_ref, 0)
@@ -141,7 +155,7 @@
         below_ref[z] = v[RAD + z]
         above_ref[z] = v[planes - 2 * RAD + z]
     if not last:
-        smear_planes(out_ref, unext_ref, taps_of(kernel_ref, 2), RAD, planes - 2 * RAD)
+        smear_planes(out_ref, unext_ref, band_ref, RAD, planes - 2 * RAD)
 
 
 def edge_kernel(last, *refs):
@@ -150,7 +164,7 @@
     if last:
         d_ref, _, whole_ref, dev_ref, v, out_ref, sems = refs[8:]
     else:
-        out_ref, unext_ref, dev_ref, v = refs[8:]
+        band_ref, out_ref, unext_ref, dev_ref, v = refs[8:]
     have, height, length = p_ref.shape
     kz = taps_of(kernel_ref, 1)
     dev_ref[...] = jnp.zeros_like(dev_ref)
@@ -178,7 +192,7 @@
             copy.start()
             copies.append(copy)
         else:
-            smear_planes(out_ref, unext_ref, taps_of(kernel_ref, 2), first, RAD)
+            smear_planes(out_ref, unext_ref, band_ref, first, RAD)
     for copy in copies:
         copy.wait()
 
@@ -235,7 +249,8 @@
             name=name,
         )(kernel, *args)
 
-    (u,) = call(first_kernel, [whole], [d], name="first")
+    band = band_of(kernel[2], length)
+    (u,) = call(first_kernel, [whole], [d, band], name="first")
     p = p_rims = d
     u_rims = u
     devs = []
@@ -251,11 +266,11 @@
             yfirst = jnp.concatenate([part[:, :RAD] for part in parts], axis=0)
         ylo = from_neighbour(yend, "gy", -1)
         yhi = from_neighbour(yfirst, "gy", 1)
-        vtop, vbot, tail = call(functools.partial(rim_kernel, iteration == 0), [rim, rim, tails], [u_rims, ylo, yhi], name="rim")
+        vtop, vbot, tail = call(functools.partial(rim_kernel, iteration == 0), [rim, rim, tails], [u_rims, ylo, yhi] + ([band] if iteration == 0 else []), name="rim")
         zlo = from_neighbour(vbot, "gz", -1)
         zhi = from_neighbour(vtop, "gz", 1)
         state = [whole] if last else [whole, whole]
-        extra = [d] if last else []
+        extra = [d] if last else [band]
         outs = call(
             functools.partial(inner_kernel, last),
             state + [dev_shape, rim, rim],
@@ -273,7 +288,7 @@
         else:
             p, u = fresh
             p_rims, u_rims, edge_dev = call(
-                functools.partial(edge_kernel, False), [rims, rims, dev_shape], args, edge_v, "edge"
+                functools.partial(edge_kernel, False), [rims, rims, dev_shape], args + [band], edge_v, "edge"
             )
         devs.append(jnp.maximum(dev, edge_dev))
     local = jnp.max(jnp.stack(devs), axis=(1, 2))

time: 135 us -> 125 us (0.926)
  Pallas kernels: 61.2 us -> 43.5 us
  other arithmetic: 2.38 us -> 7.64 us
  starting transfers between devices: 49.4 us -> 52.7 us
  local copies, waits for them, and re-layouts: 3.53 us -> 2.04 us
    pallas_call x10, Pallas kernels: 61.2 us -> 43.5 us  [call(): pl.pallas_call(body, out_shape=outs, in_specs=in_specs, out_specs=out_spe...]
    ppermute x12, starting transfers between devices: 34.9 us -> 41.4 us  [from_neighbour(): return lax.ppermute(block, axis, pairs)]
    convert_element_type x0 -> x1, other arithmetic: none -> 5.08 us  [band_of(): high.astype(jnp.bfloat16)]
    ppermute x5, starting transfers between devices: 14.5 us -> 11.3 us  [max_over(): value = jnp.maximum(value, lax.ppermute(value, axis, pairs))]
    unnamed x4 -> x2, local copies, waits for them, and re-layouts: 2.17 us -> 0.01 us
  transfers between devices with their start and end apart: 17 -> 17, of which waited for: 9 -> 9; matrix products, arithmetic and copies ran while one was open for 1% -> 6% of each run, Pallas kernels for 30% -> 23%
where the time goes in v4:
time: 125 us; the launch traced here: 124 us
  starting transfers between devices  52.7 us (42%)
  Pallas kernels  43.5 us (35%)
  waiting for transfers between devices  17.5 us (14%)
  other arithmetic  7.64 us (6%)
  local copies, waits for them, and re-layouts  2.04 us (2%)
    pallas_call x10, Pallas kernels, call(): pl.pallas_call(body, out_shape=outs, in_specs=in_specs, out_specs=out_spe...  43.5 us
    ppermute x12, starting transfers between devices, from_neighbour(): return lax.ppermute(block, axis, pairs)  41.4 us
    ppermute x5, starting transfers between devices, max_over(): value = jnp.maximum(value, lax.ppermute(value, axis, pairs))  11.3 us
    ppermute x5, waiting for transfers between devices, max_over(): value = jnp.maximum(value, lax.ppermute(value, axis, pairs))  11 us
    ppermute x12, waiting for transfers between devices, from_neighbour(): return lax.ppermute(block, axis, pairs)  6.51 us
    convert_element_type x1, other arithmetic, band_of(): high.astype(jnp.bfloat16)  5.08 us
  transfers between devices with their start and end apart: 17, of which 9 were waited for; matrix products, arithmetic and copies ran while one was open for 6% of the time, Pallas kernels for 23%

profile of v4, /device:TPU:0, one launch (start us, length us, event | category | flops | bytes accessed | tf_op | source)
XLA Modules:
  0.0 124.3 jit_solution(4122378199067807425)
XLA Ops:
  0.6 1.2 fusion.10
  1.8 5.0 %collective-permute-start = (f32[20,3,640]{2,1,0:T(4,128)S(1)}, f32[20,3,640]{2,1,0:T(4,128)S(1)}, u32[]{:S(2)}, u32[]{:S(2)}) collective-permute-start(f32[20,3,640]{2,1,0:T(4,128)S(1)} %get-tuple-element.69), channel_id=1, source_target_pairs={{0,8},{8,16},{16,24},{1,9},{9,17},{17,25},{2,10},{10,18},{18,26},{... | collective-permute-start | bytes 460808 | tf_op jit(solution)/shard_map/ppermute | solution.py:203
  6.8 1.3 %collective-permute-start.1 = (f32[20,3,640]{2,1,0:T(4,128)S(1)}, f32[20,3,640]{2,1,0:T(4,128)S(1)}, u32[]{:S(2)}, u32[]{:S(2)}) collective-permute-start(f32[20,3,640]{2,1,0:T(4,128)S(1)} %get-tuple-element.68), channel_id=1, source_target_pairs={{8,0},{16,8},{24,16},{9,1},{17,9},{25,17},{10,2},{18,10},{26,18},{... | collective-permute-start | bytes 460808 | tf_op jit(solution)/shard_map/ppermute | solution.py:203
  8.1 0.8 reduce_sum.9
  8.9 0.8 broadcast_divide_fusion.kernel_ref.refs_0_
  9.7 0.7 fusion.13
  10.3 0.0 copy-start
  10.3 5.1 %reduce-precision_convert_fusion = (bf16[1,640,640]{2,1,0:T(8,128)(2,1)S(1)}, bf16[1,640,640]{2,1,0:T(8,128)(2,1)S(1)}) fusion(f32[]{:T(128)} %bitcast.7, f32[]{:T(128)} %bitcast.6, f32[]{:T(128)} %bitcast.5, f32[]{:T(128)} %bitcast.4, f32[]{:T(128)} %bitcast.3, f32[]{:T(128)} %bitcast.2, f32[]{:T(128)} %bitcast.1), kind=kLoop, calls=%fused_computation.1 | loop fusion | flops 7782400 | bytes 1638428 | tf_op jit(solution)/shard_map/convert_element_type | solution.py:36
  15.4 0.2 pad_maximum_fusion.band_ref.refs_0_.refs_6_.refs_8_
  15.6 0.0 copy-done
  15.6 4.4 %first.1.u_ref.refs_2_ = f32[20,80,640]{2,1,0:T(8,128)S(1)} custom-call(f32[3,7]{1,0:T(4,128)S(1)} %broadcast_divide_fusion.kernel_ref.refs_0_, f32[20,80,640]{2,1,0:T(8,128)S(1)} %bitcast.16, bf16[2,640,640]{2,1,0:T(8,128)(2,1)S(1)} %pad_maximum_fusion.band_ref.refs_0_.refs_6_.refs_8_), custom_call_target="tpu_custom_call" | custom-call | tf_op jit(solution)/shard_map/first/pallas_call | solution.py:241
  20.0 0.0 collective-permute-done.ylo_ref
  20.0 0.0 collective-permute-done.1.yhi_ref
  20.0 3.1 %rim.3 = (f32[3,80,640]{2,1,0:T(8,128)S(1)}, f32[3,80,640]{2,1,0:T(8,128)S(1)}, f32[20,8,640]{2,1,0:T(8,128)S(1)}) custom-call(f32[3,7]{1,0:T(4,128)S(1)} %broadcast_divide_fusion.kernel_ref.refs_0_, f32[20,80,640]{2,1,0:T(8,128)S(1)} %first.1.u_ref.refs_2_, f32[20,3,640]{2,1,0:T(4,128)S(1)} %collective-permute-done.ylo_ref, ...), custom_call_target="tpu_custom_call" | custom-call | tf_op jit(solution)/shard_map/rim/pallas_call | solution.py:241
  23.1 1.5 %collective-permute-start.2 = (f32[3,80,640]{2,1,0:T(8,128)S(1)}, f32[3,80,640]{2,1,0:T(8,128)S(1)}, u32[]{:S(2)}, u32[]{:S(2)}) collective-permute-start(f32[3,80,640]{2,1,0:T(8,128)S(1)} %get-tuple-element.33.refs_5_), channel_id=1, source_target_pairs={{0,1},{1,2},{2,3},{3,4},{4,5},{5,6},{6,7},{8,9},{9,10},{10,11},{11... | collective-permute-start | bytes 1843208 | tf_op jit(solution)/shard_map/ppermute | solution.py:203
  24.6 1.3 %collective-permute-start.3 = (f32[3,80,640]{2,1,0:T(8,128)S(1)}, f32[3,80,640]{2,1,0:T(8,128)S(1)}, u32[]{:S(2)}, u32[]{:S(2)}) collective-permute-start(f32[3,80,640]{2,1,0:T(8,128)S(1)} %get-tuple-element.34.refs_4_), channel_id=1, source_target_pairs={{1,0},{2,1},{3,2},{4,3},{5,4},{6,5},{7,6},{9,8},{10,9},{11,10},{12... | collective-permute-start | bytes 1843208 | tf_op jit(solution)/shard_map/ppermute | solution.py:203
  25.9 8.1 %inner.3 = (f32[20,80,640]{2,1,0:T(8,128)S(1)}, f32[20,80,640]{2,1,0:T(8,128)S(1)}, f32[8,128]{1,0:T(8,128)S(1)}, f32[3,80,640]{2,1,0:T(8,128)S(1)}, f32[3,80,640]{2,1,0:T(8,128)S(1)}) custom-call(f32[3,7]{1,0:T(4,128)S(1)} %broadcast_divide_fusion.kernel_ref.refs_0_, f32[20,80,640]{2,1,0:T(8,128)S(1)} %bitcast.17, f32[20,80,640]{2,1,0:T(8,128)S(1)} %first.1.u_ref.refs_2_, ...), custom_call_target="tpu_custom_call" | custom-call | tf_op jit(solution)/shard_map/inner/pallas_call | solution.py:241
  34.0 0.1 fusion.9
  34.0 0.0 collective-permute-done.2.refs_2_
  34.1 0.0 collective-permute-done.3.refs_3_
  34.1 3.1 %edge.3 = (f32[6,80,640]{2,1,0:T(8,128)S(1)}, f32[6,80,640]{2,1,0:T(8,128)S(1)}, f32[8,128]{1,0:T(8,128)S(1)}) custom-call(f32[3,7]{1,0:T(4,128)S(1)} %broadcast_divide_fusion.kernel_ref.refs_0_, f32[20,80,640]{2,1,0:T(8,128)S(1)} %bitcast.18, f32[3,80,640]{2,1,0:T(8,128)S(1)} %collective-permute-done.2.refs_2_, ...), custom_call_target="tpu_custom_call" | custom-call | tf_op jit(solution)/shard_map/edge/pallas_call | solution.py:241
  37.3 1.3 %collective-permute-start.5 = (f32[20,3,640]{2,1,0:T(4,128)S(1)}, f32[20,3,640]{2,1,0:T(4,128)S(1)}, u32[]{:S(2)}, u32[]{:S(2)}) collective-permute-start(f32[20,3,640]{2,1,0:T(4,128)S(1)} %pad_maximum_fusion.2), channel_id=1, source_target_pairs={{8,0},{16,8},{24,16},{9,1},{17,9},{25,17},{10,2},{18,10},{26,18},{... | collective-permute-start | bytes 460808 | tf_op jit(solution)/shard_map/ppermute | solution.py:203
  38.6 5.0 %collective-permute-start.4 = (f32[20,3,640]{2,1,0:T(4,128)S(1)}, f32[20,3,640]{2,1,0:T(4,128)S(1)}, u32[]{:S(2)}, u32[]{:S(2)}) collective-permute-start(f32[20,3,640]{2,1,0:T(4,128)S(1)} %pad_maximum_fusion.1), channel_id=1, source_target_pairs={{0,8},{8,16},{16,24},{1,9},{9,17},{17,25},{2,10},{10,18},{18,26},{... | collective-permute-start | bytes 460808 | tf_op jit(solution)/shard_map/ppermute | solution.py:203
  43.6 1.7 %collective-permute-done.5.yhi_ref = f32[20,3,640]{2,1,0:T(4,128)S(1)} collective-permute-done((f32[20,3,640]{2,1,0:T(4,128)S(1)}, f32[20,3,640]{2,1,0:T(4,128)S(1)}, u32[]{:S(2)}, u32[]{:S(2)}) %collective-permute-start.5) | collective-permute-done | bytes 153632 | tf_op jit(solution)/shard_map/ppermute | solution.py:203
  45.4 1.5 %collective-permute-done.4.ylo_ref = f32[20,3,640]{2,1,0:T(4,128)S(1)} collective-permute-done((f32[20,3,640]{2,1,0:T(4,128)S(1)}, f32[20,3,640]{2,1,0:T(4,128)S(1)}, u32[]{:S(2)}, u32[]{:S(2)}) %collective-permute-start.4) | collective-permute-done | bytes 153632 | tf_op jit(solution)/shard_map/ppermute | solution.py:203
  46.9 1.7 %rim.4 = (f32[3,80,640]{2,1,0:T(8,128)S(1)}, f32[3,80,640]{2,1,0:T(8,128)S(1)}, f32[20,8,640]{2,1,0:T(8,128)S(1)}) custom-call(f32[3,7]{1,0:T(4,128)S(1)} %broadcast_divide_fusion.kernel_ref.refs_0_, f32[6,80,640]{2,1,0:T(8,128)S(1)} %get-tuple-element.39.u_ref, f32[20,3,640]{2,1,0:T(4,128)S(1)} %collective-permute-done.4.ylo_ref, ...), custom_call_target="tpu_custom_call" | custom-call | tf_op jit(solution)/shard_map/rim/pallas_call | solution.py:241
  48.6 9.1 %collective-permute-start.6 = (f32[3,80,640]{2,1,0:T(8,128)S(1)}, f32[3,80,640]{2,1,0:T(8,128)S(1)}, u32[]{:S(2)}, u32[]{:S(2)}) collective-permute-start(f32[3,80,640]{2,1,0:T(8,128)S(1)} %get-tuple-element.41.refs_5_), channel_id=1, source_target_pairs={{0,1},{1,2},{2,3},{3,4},{4,5},{5,6},{6,7},{8,9},{9,10},{10,11},{11... | collective-permute-start | bytes 1843208 | tf_op jit(solution)/shard_map/ppermute | solution.py:203
  57.7 1.3 %collective-permute-start.7 = (f32[3,80,640]{2,1,0:T(8,128)S(1)}, f32[3,80,640]{2,1,0:T(8,128)S(1)}, u32[]{:S(2)}, u32[]{:S(2)}) collective-permute-start(f32[3,80,640]{2,1,0:T(8,128)S(1)} %get-tuple-element.42.refs_4_), channel_id=1, source_target_pairs={{1,0},{2,1},{3,2},{4,3},{5,4},{6,5},{7,6},{9,8},{10,9},{11,10},{12... | collective-permute-start | bytes 1843208 | tf_op jit(solution)/shard_map/ppermute | solution.py:203
  59.0 8.1 %inner.4 = (f32[20,80,640]{2,1,0:T(8,128)S(1)}, f32[20,80,640]{2,1,0:T(8,128)S(1)}, f32[8,128]{1,0:T(8,128)S(1)}, f32[3,80,640]{2,1,0:T(8,128)S(1)}, f32[3,80,640]{2,1,0:T(8,128)S(1)}) custom-call(f32[3,7]{1,0:T(4,128)S(1)} %broadcast_divide_fusion.kernel_ref.refs_0_, f32[20,80,640]{2,1,0:T(8,128)S(1)} %get-tuple-element.43.refs_1_, ...), custom_call_target="tpu_custom_call" | custom-call | tf_op jit(solution)/shard_map/inner/pallas_call | solution.py:241
  67.1 0.1 fusion.8
  67.2 0.0 collective-permute-done.6.refs_2_
  67.2 0.0 collective-permute-done.7.refs_3_
  67.2 3.1 %edge.4 = (f32[6,80,640]{2,1,0:T(8,128)S(1)}, f32[6,80,640]{2,1,0:T(8,128)S(1)}, f32[8,128]{1,0:T(8,128)S(1)}) custom-call(f32[3,7]{1,0:T(4,128)S(1)} %broadcast_divide_fusion.kernel_ref.refs_0_, f32[6,80,640]{2,1,0:T(8,128)S(1)} %get-tuple-element.38.refs_1_, f32[3,80,640]{2,1,0:T(8,128)S(1)} %collective-permute-done.6.refs_2_, ...), custom_call_target="tpu_custom_call" | custom-call | tf_op jit(solution)/shard_map/edge/pallas_call | solution.py:241
  70.4 1.3 %collective-permute-start.9 = (f32[20,3,640]{2,1,0:T(4,128)S(1)}, f32[20,3,640]{2,1,0:T(4,128)S(1)}, u32[]{:S(2)}, u32[]{:S(2)}) collective-permute-start(f32[20,3,640]{2,1,0:T(4,128)S(1)} %pad_maximum_fusion.4), channel_id=1, source_target_pairs={{8,0},{16,8},{24,16},{9,1},{17,9},{25,17},{10,2},{18,10},{26,18},{... | collective-permute-start | bytes 460808 | tf_op jit(solution)/shard_map/ppermute | solution.py:203
  71.8 4.7 %collective-permute-start.8 = (f32[20,3,640]{2,1,0:T(4,128)S(1)}, f32[20,3,640]{2,1,0:T(4,128)S(1)}, u32[]{:S(2)}, u32[]{:S(2)}) collective-permute-start(f32[20,3,640]{2,1,0:T(4,128)S(1)} %pad_maximum_fusion.3), channel_id=1, source_target_pairs={{0,8},{8,16},{16,24},{1,9},{9,17},{17,25},{2,10},{10,18},{18,26},{... | collective-permute-start | bytes 460808 | tf_op jit(solution)/shard_map/ppermute | solution.py:203
  76.5 1.7 %collective-permute-done.9.yhi_ref = f32[20,3,640]{2,1,0:T(4,128)S(1)} collective-permute-done((f32[20,3,640]{2,1,0:T(4,128)S(1)}, f32[20,3,640]{2,1,0:T(4,128)S(1)}, u32[]{:S(2)}, u32[]{:S(2)}) %collective-permute-start.9) | collective-permute-done | bytes 153632 | tf_op jit(solution)/shard_map/ppermute | solution.py:203
  78.2 1.5 %collective-permute-done.8.ylo_ref = f32[20,3,640]{2,1,0:T(4,128)S(1)} collective-permute-done((f32[20,3,640]{2,1,0:T(4,128)S(1)}, f32[20,3,640]{2,1,0:T(4,128)S(1)}, u32[]{:S(2)}, u32[]{:S(2)}) %collective-permute-start.8) | collective-permute-done | bytes 153632 | tf_op jit(solution)/shard_map/ppermute | solution.py:203
  79.8 1.7 %rim.5 = (f32[3,80,640]{2,1,0:T(8,128)S(1)}, f32[3,80,640]{2,1,0:T(8,128)S(1)}, f32[20,8,640]{2,1,0:T(8,128)S(1)}) custom-call(f32[3,7]{1,0:T(4,128)S(1)} %broadcast_divide_fusion.kernel_ref.refs_0_, f32[6,80,640]{2,1,0:T(8,128)S(1)} %get-tuple-element.48.u_ref, f32[20,3,640]{2,1,0:T(4,128)S(1)} %collective-permute-done.8.ylo_ref, ...), custom_call_target="tpu_custom_call" | custom-call | tf_op jit(solution)/shard_map/rim/pallas_call | solution.py:241
  81.5 8.3 %collective-permute-start.10 = (f32[3,80,640]{2,1,0:T(8,128)S(1)}, f32[3,80,640]{2,1,0:T(8,128)S(1)}, u32[]{:S(2)}, u32[]{:S(2)}) collective-permute-start(f32[3,80,640]{2,1,0:T(8,128)S(1)} %get-tuple-element.50.refs_5_), channel_id=1, source_target_pairs={{0,1},{1,2},{2,3},{3,4},{4,5},{5,6},{6,7},{8,9},{9,10},{10,11},{11... | collective-permute-start | bytes 1843208 | tf_op jit(solution)/shard_map/ppermute | solution.py:203
  89.8 1.3 %collective-permute-start.11 = (f32[3,80,640]{2,1,0:T(8,128)S(1)}, f32[3,80,640]{2,1,0:T(8,128)S(1)}, u32[]{:S(2)}, u32[]{:S(2)}) collective-permute-start(f32[3,80,640]{2,1,0:T(8,128)S(1)} %get-tuple-element.51.refs_4_), channel_id=1, source_target_pairs={{1,0},{2,1},{3,2},{4,3},{5,4},{6,5},{7,6},{9,8},{10,9},{11,10},{12... | collective-permute-start | bytes 1843208 | tf_op jit(solution)/shard_map/ppermute | solution.py:203
  91.1 7.6 %inner.5 = (f32[20,80,640]{2,1,0:T(8,128)}, f32[8,128]{1,0:T(8,128)S(1)}, f32[3,80,640]{2,1,0:T(8,128)S(1)}, f32[3,80,640]{2,1,0:T(8,128)S(1)}) custom-call(f32[3,7]{1,0:T(4,128)S(1)} %broadcast_divide_fusion.kernel_ref.refs_0_, f32[20,80,640]{2,1,0:T(8,128)S(1)} %get-tuple-element.52.refs_1_, f32[20,80,640]{2,1,0:T(8,128)S(1)} %get-tuple-element.49.refs_2_, ...), custom_call_target="tpu_custom_call" | custom-call | tf_op jit(solution)/shard_map/inner/pallas_call | solution.py:241
  98.7 0.0 collective-permute-done.10.refs_2_
  98.7 0.0 collective-permute-done.11.refs_3_
  98.7 2.7 %edge.5 = (f32[20,80,640]{2,1,0:T(8,128)}, f32[8,128]{1,0:T(8,128)S(1)}) custom-call(f32[3,7]{1,0:T(4,128)S(1)} %broadcast_divide_fusion.kernel_ref.refs_0_, f32[6,80,640]{2,1,0:T(8,128)S(1)} %get-tuple-element.47.refs_1_, f32[3,80,640]{2,1,0:T(8,128)S(1)} %collective-permute-done.10.refs_2_, ...), custom_call_target="tpu_custom_call", output_to_operand_aliasing={{0}: (9, {})} | custom-call | tf_op jit(solution)/shard_map/edge/pallas_call | solution.py:241
  101.4 0.1 maximum_reduce_fusion
  101.5 5.4 %collective-permute-start.12 = (f32[3]{0:T(128)S(1)}, f32[3]{0:T(128)S(1)}, u32[]{:S(2)}, u32[]{:S(2)}) collective-permute-start(f32[3]{0:T(128)S(1)} %maximum_reduce_fusion), channel_id=1, source_target_pairs={{0,1},{1,0},{2,3},{3,2},{4,5},{5,4},{6,7},{7,6},{8,9},{9,8},{10,11... | collective-permute-start | bytes 44 | tf_op jit(solution)/shard_map/ppermute | solution.py:214
  106.9 0.8 collective-permute-done.12
  107.7 0.1 collective-permute-start.13
  107.8 3.5 %collective-permute-done.13 = f32[3]{0:T(128)S(1)} collective-permute-done((f32[3]{0:T(128)S(1)}, f32[3]{0:T(128)S(1)}, u32[]{:S(2)}, u32[]{:S(2)}) %collective-permute-start.13) | collective-permute-done | bytes 44 | tf_op jit(solution)/shard_map/ppermute | solution.py:214
  111.3 0.0 collective-permute-start.14
  111.3 3.6 %collective-permute-done.14 = f32[3]{0:T(128)S(1)} collective-permute-done((f32[3]{0:T(128)S(1)}, f32[3]{0:T(128)S(1)}, u32[]{:S(2)}, u32[]{:S(2)}) %collective-permute-start.14) | collective-permute-done | bytes 44 | tf_op jit(solution)/shard_map/ppermute | solution.py:214
  114.8 2.5 %collective-permute-start.15 = (f32[3]{0:T(128)S(1)}, f32[3]{0:T(128)S(1)}, u32[]{:S(2)}, u32[]{:S(2)}) collective-permute-start(f32[3]{0:T(128)S(1)} %max.29), channel_id=1, source_target_pairs={{0,8},{8,0},{16,24},{24,16},{1,9},{9,1},{17,25},{25,17},{2,10},{10... | collective-permute-start | bytes 44 | tf_op jit(solution)/shard_map/ppermute | solution.py:214
  117.3 1.5 %collective-permute-done.15 = f32[3]{0:T(128)S(1)} collective-permute-done((f32[3]{0:T(128)S(1)}, f32[3]{0:T(128)S(1)}, u32[]{:S(2)}, u32[]{:S(2)}) %collective-permute-start.15) | collective-permute-done | bytes 44 | tf_op jit(solution)/shard_map/ppermute | solution.py:214
  118.9 3.3 %collective-permute-start.16 = (f32[3]{0:T(128)S(1)}, f32[3]{0:T(128)S(1)}, u32[]{:S(2)}, u32[]{:S(2)}) collective-permute-start(f32[3]{0:T(128)S(1)} %max.30), channel_id=1, source_target_pairs={{0,16},{8,24},{16,0},{24,8},{1,17},{9,25},{17,1},{25,9},{2,18},{10... | collective-permute-start | bytes 44 | tf_op jit(solution)/shard_map/ppermute | solution.py:214
  122.2 1.5 %collective-permute-done.16 = f32[3]{0:T(128)S(1)} collective-permute-done((f32[3]{0:T(128)S(1)}, f32[3]{0:T(128)S(1)}, u32[]{:S(2)}, u32[]{:S(2)}) %collective-permute-start.16) | collective-permute-done | bytes 44 | tf_op jit(solution)/shard_map/ppermute | solution.py:214
  123.8 0.5 max.31
  (13 shorter events, 0.3 us)
Async XLA Ops:
  1.8 18.2 %collective-permute-start = (f32[20,3,640]{2,1,0:T(4,128)S(1)}, f32[20,3,640]{2,1,0:T(4,128)S(1)}, u32[]{:S(2)}, u32[]{:S(2)}) collective-permute-start(f32[20,3,640]{2,1,0:T(4,128)S(1)} %get-tuple-element.69), channel_id=1, source_target_pairs={{0,8},{8,16},{16,24},{1,9},{9,17},{17,25},{2,10},{10,18},{18,26},{... | collective-permute-start | bytes 460808 | tf_op jit(solution)/shard_map/ppermute | solution.py:203
  6.8 13.2 %collective-permute-start.1 = (f32[20,3,640]{2,1,0:T(4,128)S(1)}, f32[20,3,640]{2,1,0:T(4,128)S(1)}, u32[]{:S(2)}, u32[]{:S(2)}) collective-permute-start(f32[20,3,640]{2,1,0:T(4,128)S(1)} %get-tuple-element.68), channel_id=1, source_target_pairs={{8,0},{16,8},{24,16},{9,1},{17,9},{25,17},{10,2},{18,10},{26,18},{... | collective-permute-start | bytes 460808 | tf_op jit(solution)/shard_map/ppermute | solution.py:203
  10.3 5.3 %copy-start = (f32[80,20,640]{2,0,1:T(8,128)S(1)}, f32[80,20,640]{2,0,1:T(8,128)}, u32[]{:S(2)}) copy-start(f32[80,20,640]{2,0,1:T(8,128)} %param.2) | copy-start | bytes 12288004
  23.1 10.9 %collective-permute-start.2 = (f32[3,80,640]{2,1,0:T(8,128)S(1)}, f32[3,80,640]{2,1,0:T(8,128)S(1)}, u32[]{:S(2)}, u32[]{:S(2)}) collective-permute-start(f32[3,80,640]{2,1,0:T(8,128)S(1)} %get-tuple-element.33.refs_5_), channel_id=1, source_target_pairs={{0,1},{1,2},{2,3},{3,4},{4,5},{5,6},{6,7},{8,9},{9,10},{10,11},{11... | collective-permute-start | bytes 1843208 | tf_op jit(solution)/shard_map/ppermute | solution.py:203
  24.6 9.4 %collective-permute-start.3 = (f32[3,80,640]{2,1,0:T(8,128)S(1)}, f32[3,80,640]{2,1,0:T(8,128)S(1)}, u32[]{:S(2)}, u32[]{:S(2)}) collective-permute-start(f32[3,80,640]{2,1,0:T(8,128)S(1)} %get-tuple-element.34.refs_4_), channel_id=1, source_target_pairs={{1,0},{2,1},{3,2},{4,3},{5,4},{6,5},{7,6},{9,8},{10,9},{11,10},{12... | collective-permute-start | bytes 1843208 | tf_op jit(solution)/shard_map/ppermute | solution.py:203
  37.3 8.1 %collective-permute-start.5 = (f32[20,3,640]{2,1,0:T(4,128)S(1)}, f32[20,3,640]{2,1,0:T(4,128)S(1)}, u32[]{:S(2)}, u32[]{:S(2)}) collective-permute-start(f32[20,3,640]{2,1,0:T(4,128)S(1)} %pad_maximum_fusion.2), channel_id=1, source_target_pairs={{8,0},{16,8},{24,16},{9,1},{17,9},{25,17},{10,2},{18,10},{26,18},{... | collective-permute-start | bytes 460808 | tf_op jit(solution)/shard_map/ppermute | solution.py:203
  38.6 8.3 %collective-permute-start.4 = (f32[20,3,640]{2,1,0:T(4,128)S(1)}, f32[20,3,640]{2,1,0:T(4,128)S(1)}, u32[]{:S(2)}, u32[]{:S(2)}) collective-permute-start(f32[20,3,640]{2,1,0:T(4,128)S(1)} %pad_maximum_fusion.1), channel_id=1, source_target_pairs={{0,8},{8,16},{16,24},{1,9},{9,17},{17,25},{2,10},{10,18},{18,26},{... | collective-permute-start | bytes 460808 | tf_op jit(solution)/shard_map/ppermute | solution.py:203
  48.6 18.6 %collective-permute-start.6 = (f32[3,80,640]{2,1,0:T(8,128)S(1)}, f32[3,80,640]{2,1,0:T(8,128)S(1)}, u32[]{:S(2)}, u32[]{:S(2)}) collective-permute-start(f32[3,80,640]{2,1,0:T(8,128)S(1)} %get-tuple-element.41.refs_5_), channel_id=1, source_target_pairs={{0,1},{1,2},{2,3},{3,4},{4,5},{5,6},{6,7},{8,9},{9,10},{10,11},{11... | collective-permute-start | bytes 1843208 | tf_op jit(solution)/shard_map/ppermute | solution.py:203
  57.7 9.4 %collective-permute-start.7 = (f32[3,80,640]{2,1,0:T(8,128)S(1)}, f32[3,80,640]{2,1,0:T(8,128)S(1)}, u32[]{:S(2)}, u32[]{:S(2)}) collective-permute-start(f32[3,80,640]{2,1,0:T(8,128)S(1)} %get-tuple-element.42.refs_4_), channel_id=1, source_target_pairs={{1,0},{2,1},{3,2},{4,3},{5,4},{6,5},{7,6},{9,8},{10,9},{11,10},{12... | collective-permute-start | bytes 1843208 | tf_op jit(solution)/shard_map/ppermute | solution.py:203
  70.4 7.8 %collective-permute-start.9 = (f32[20,3,640]{2,1,0:T(4,128)S(1)}, f32[20,3,640]{2,1,0:T(4,128)S(1)}, u32[]{:S(2)}, u32[]{:S(2)}) collective-permute-start(f32[20,3,640]{2,1,0:T(4,128)S(1)} %pad_maximum_fusion.4), channel_id=1, source_target_pairs={{8,0},{16,8},{24,16},{9,1},{17,9},{25,17},{10,2},{18,10},{26,18},{... | collective-permute-start | bytes 460808 | tf_op jit(solution)/shard_map/ppermute | solution.py:203
  71.8 8.0 %collective-permute-start.8 = (f32[20,3,640]{2,1,0:T(4,128)S(1)}, f32[20,3,640]{2,1,0:T(4,128)S(1)}, u32[]{:S(2)}, u32[]{:S(2)}) collective-permute-start(f32[20,3,640]{2,1,0:T(4,128)S(1)} %pad_maximum_fusion.3), channel_id=1, source_target_pairs={{0,8},{8,16},{16,24},{1,9},{9,17},{17,25},{2,10},{10,18},{18,26},{... | collective-permute-start | bytes 460808 | tf_op jit(solution)/shard_map/ppermute | solution.py:203
  81.5 17.2 %collective-permute-start.10 = (f32[3,80,640]{2,1,0:T(8,128)S(1)}, f32[3,80,640]{2,1,0:T(8,128)S(1)}, u32[]{:S(2)}, u32[]{:S(2)}) collective-permute-start(f32[3,80,640]{2,1,0:T(8,128)S(1)} %get-tuple-element.50.refs_5_), channel_id=1, source_target_pairs={{0,1},{1,2},{2,3},{3,4},{4,5},{5,6},{6,7},{8,9},{9,10},{10,11},{11... | collective-permute-start | bytes 1843208 | tf_op jit(solution)/shard_map/ppermute | solution.py:203
  89.8 8.9 %collective-permute-start.11 = (f32[3,80,640]{2,1,0:T(8,128)S(1)}, f32[3,80,640]{2,1,0:T(8,128)S(1)}, u32[]{:S(2)}, u32[]{:S(2)}) collective-permute-start(f32[3,80,640]{2,1,0:T(8,128)S(1)} %get-tuple-element.51.refs_4_), channel_id=1, source_target_pairs={{1,0},{2,1},{3,2},{4,3},{5,4},{6,5},{7,6},{9,8},{10,9},{11,10},{12... | collective-permute-start | bytes 1843208 | tf_op jit(solution)/shard_map/ppermute | solution.py:203
  101.5 6.2 %collective-permute-start.12 = (f32[3]{0:T(128)S(1)}, f32[3]{0:T(128)S(1)}, u32[]{:S(2)}, u32[]{:S(2)}) collective-permute-start(f32[3]{0:T(128)S(1)} %maximum_reduce_fusion), channel_id=1, source_target_pairs={{0,1},{1,0},{2,3},{3,2},{4,5},{5,4},{6,7},{7,6},{8,9},{9,8},{10,11... | collective-permute-start | bytes 44 | tf_op jit(solution)/shard_map/ppermute | solution.py:214
  107.7 3.6 %collective-permute-start.13 = (f32[3]{0:T(128)S(1)}, f32[3]{0:T(128)S(1)}, u32[]{:S(2)}, u32[]{:S(2)}) collective-permute-start(f32[3]{0:T(128)S(1)} %max.27), channel_id=1, source_target_pairs={{0,2},{1,3},{2,0},{3,1},{4,6},{5,7},{6,4},{7,5},{8,10},{9,11},{10,... | collective-permute-start | bytes 44 | tf_op jit(solution)/shard_map/ppermute | solution.py:214
  111.3 3.6 %collective-permute-start.14 = (f32[3]{0:T(128)S(1)}, f32[3]{0:T(128)S(1)}, u32[]{:S(2)}, u32[]{:S(2)}) collective-permute-start(f32[3]{0:T(128)S(1)} %max.28), channel_id=1, source_target_pairs={{0,4},{1,5},{2,6},{3,7},{4,0},{5,1},{6,2},{7,3},{8,12},{9,13},{10,... | collective-permute-start | bytes 44 | tf_op jit(solution)/shard_map/ppermute | solution.py:214
  114.8 4.0 %collective-permute-start.15 = (f32[3]{0:T(128)S(1)}, f32[3]{0:T(128)S(1)}, u32[]{:S(2)}, u32[]{:S(2)}) collective-permute-start(f32[3]{0:T(128)S(1)} %max.29), channel_id=1, source_target_pairs={{0,8},{8,0},{16,24},{24,16},{1,9},{9,1},{17,25},{25,17},{2,10},{10... | collective-permute-start | bytes 44 | tf_op jit(solution)/shard_map/ppermute | solution.py:214
  118.9 4.9 %collective-permute-start.16 = (f32[3]{0:T(128)S(1)}, f32[3]{0:T(128)S(1)}, u32[]{:S(2)}, u32[]{:S(2)}) collective-permute-start(f32[3]{0:T(128)S(1)} %max.30), channel_id=1, source_target_pairs={{0,16},{8,24},{16,0},{24,8},{1,17},{9,25},{17,1},{25,9},{2,18},{10... | collective-permute-start | bytes 44 | tf_op jit(solution)/shard_map/ppermute | solution.py:214
